TPU v7x, 512 devices: a whole 4x4x16 slice. The times are simulated.
512 devices in a mesh: region: 8 (over x, core), dev: 64 (over z, y).
Axes of the slice: x: 4, y: 4, z: 16, core: 2. Of those that a mesh axis runs over, the one named last changes fastest.
Arguments:
- positions: float32 [3, 2048, 128], P(None, ('region', 'dev')), as said below
- charges: float32 [2048, 128], P(('region', 'dev')), may hold values from -3 to 3
- types: int32 [2048, 128], P(('region', 'dev')), may hold values from 0 to 5
- pairs: int32 [2048, 13], P(('region', 'dev')), may hold values from -1 to 2047, as said below
- owner_map: int32 [2048], replicated, may hold values from 0 to 2047, as said below
Outputs:
- born_radius: float32 [2048, 128], P(('region', 'dev'))
- energy: float32 [2048, 128], P(('region', 'dev'))
- forces: float32 [3, 2048, 128], P(None, ('region', 'dev'))
- born_grad: float32 [2048, 128], P(('region', 'dev'))
Inputs may be any that keep to these rules, and one draw needn't show every extreme that they name: `pairs`: row g lists cells next to block g's cell; -1 marks an empty slot. The block that owner_map gives for a listed cell differs from g and lies in g's region (blocks r * 256 to (r + 1) * 256 - 1) or in the next region. No pair of blocks is listed twice, in either order. `owner_map`: for each region r, a permutation of the cells r * 256 to (r + 1) * 256 - 1 onto the blocks with the same ids. `positions`: any two atoms are 1.5 or more apart.
All inputs are finite; a program needn't handle non-finite values.
Results may differ from a plain program's by a relative error of at most 0.0003.
Values sent between devices are 32-bit elements; how exact they have to be, the bound alone decides.
A program may use at most 64 MiB of HBM per device.

v0:
```python
import jax
import jax.numpy as jnp
from jax import lax
from jax.sharding import PartitionSpec as P

type_radii = (1.2, 1.7, 1.55, 1.52, 1.85, 1.8)
type_scales = (0.85, 0.72, 0.79, 0.85, 0.86, 0.96)
radius_offset = 0.09
born_alpha = 1.0
born_beta = 0.8
born_gamma = 4.85
solvent_tau = 1.0 - 1.0 / 78.5


def passed_along(value, axis, by):
    size = lax.axis_size(axis)
    pairs = [(i, i + by) for i in range(size) if 0 <= i + by < size]
    return lax.ppermute(value, axis, pairs)


def lookup_types(types):
    shape_tail = (-1,) + (1,) * types.ndim
    type_ids = jnp.arange(len(type_radii), dtype=jnp.int32).reshape(shape_tail)
    one_hot = (types[None] == type_ids).astype(jnp.float32)
    radii_table = jnp.asarray(type_radii, jnp.float32).reshape(shape_tail)
    scale_table = jnp.asarray(type_scales, jnp.float32).reshape(shape_tail)
    intrinsic = jnp.sum(one_hot * radii_table, axis=0)
    offset_rho = intrinsic - radius_offset
    scaled_rho = jnp.sum(one_hot * scale_table, axis=0) * offset_rho
    return (intrinsic, offset_rho, scaled_rho)


def descreen(distance, rho_self, scaled_other):
    high_edge = distance + scaled_other
    low_edge = jnp.maximum(rho_self, jnp.abs(distance - scaled_other))
    inv_low = 1.0 / low_edge
    inv_high = 1.0 / high_edge
    inv_dist = 1.0 / distance
    integral = (
        inv_low
        - inv_high
        + 0.25 * distance * (inv_high * inv_high - inv_low * inv_low)
        + 0.5 * inv_dist * jnp.log(low_edge * inv_high)
        + 0.25 * scaled_other * scaled_other * inv_dist * (inv_low * inv_low - inv_high * inv_high)
    )
    inner_term = jnp.where(
        rho_self < scaled_other - distance, 2.0 * (1.0 / rho_self - inv_low), 0.0
    )
    return jnp.where(high_edge > rho_self, 0.5 * (integral + inner_term), 0.0)


def masked_sum(values, keep_mask, reduce_axes):
    return jnp.sum(jnp.where(keep_mask, values, 0.0), axis=reduce_axes)


def pair_geometry(home_block, partner_fields, usable):
    slot_count = partner_fields.shape[1]
    atom_count = home_block.shape[-1]
    separation = home_block[:3, None, :, None] - partner_fields[:3, :, None, :]
    squared = jnp.sum(separation * separation, axis=0)
    slot_ids = jnp.arange(slot_count, dtype=jnp.int32)[:, None, None]
    atom_ids = jnp.arange(atom_count, dtype=jnp.int32)
    diagonal = (slot_ids == 0) & (atom_ids[:, None] == atom_ids[None, :])[None]
    home_mask = usable[:, None, None] & jnp.logical_not(diagonal)
    partner_mask = home_mask & (slot_ids > 0)
    distance = jnp.sqrt(jnp.where(home_mask, squared, 1.0))
    return (separation, distance, home_mask, partner_mask)


def descreen_tile(home_block, partner_fields, usable):
    separation, distance, home_mask, partner_mask = pair_geometry(
        home_block, partner_fields, usable
    )
    home_term = descreen(distance, home_block[3][None, :, None], partner_fields[4][:, None, :])
    partner_term = descreen(distance, partner_fields[3][:, None, :], home_block[4][None, :, None])
    return (
        masked_sum(home_term, home_mask, (0, 2))[None],
        masked_sum(partner_term, partner_mask, 1)[None],
    )


def energy_tile(home_block, partner_fields, usable):
    separation, distance, home_mask, partner_mask = pair_geometry(
        home_block, partner_fields, usable
    )
    charge_prod = solvent_tau * home_block[3][None, :, None] * partner_fields[3][:, None, :]
    radius_home = home_block[4][None, :, None]
    radius_partner = partner_fields[4][:, None, :]
    radius_prod = radius_home * radius_partner
    squared = distance * distance
    exponent_arg = squared / (4.0 * radius_prod)
    damped = jnp.exp(-exponent_arg)
    denom_sq = squared + radius_prod * damped
    denom_root = jnp.sqrt(denom_sq)
    inv_cube = 1.0 / (denom_root * denom_sq)
    pair_energy = -0.5 * charge_prod / denom_root
    pull_coef = -charge_prod * (1.0 - 0.25 * damped) * inv_cube
    grad_common = 0.5 * charge_prod * damped * (1.0 + exponent_arg) * inv_cube
    home_sum = jnp.stack(
        [
            masked_sum(pull_coef * separation[0], home_mask, (0, 2)),
            masked_sum(pull_coef * separation[1], home_mask, (0, 2)),
            masked_sum(pull_coef * separation[2], home_mask, (0, 2)),
            masked_sum(pair_energy, home_mask, (0, 2)),
            masked_sum(grad_common * radius_partner, home_mask, (0, 2)),
        ]
    )
    other_sum = jnp.stack(
        [
            masked_sum(-pull_coef * separation[0], partner_mask, 1),
            masked_sum(-pull_coef * separation[1], partner_mask, 1),
            masked_sum(-pull_coef * separation[2], partner_mask, 1),
            masked_sum(pair_energy, partner_mask, 1),
            masked_sum(grad_common * radius_home, partner_mask, 1),
        ]
    )
    return (home_sum, other_sum)


def import_fields(payload):
    home_slab = lax.all_gather(payload, "dev", axis=1, tiled=True)
    next_slab = passed_along(home_slab, "region", -1)
    return jnp.concatenate([home_slab, next_slab], axis=1)


def return_halves(buffer):
    region_rows = buffer.shape[1] // 2
    home_part = buffer[:, :region_rows]
    next_part = buffer[:, region_rows:]
    arrived = passed_along(next_part, "region", 1)
    return lax.psum_scatter(home_part + arrived, "dev", scatter_dimension=1, tiled=True)


def local_sweep(own_fields, imported, slot_ids, live_slot, tile_fn, field_count):
    first_ok = jnp.zeros((1,), jnp.int32) == 0

    def visit(buffer, block_index):
        home_block = jnp.take(own_fields, block_index, axis=1)
        targets = jnp.take(slot_ids, block_index, axis=0)
        usable = jnp.concatenate([first_ok, jnp.take(live_slot, block_index, axis=0)])
        partner_fields = jnp.concatenate(
            [home_block[:, None], jnp.take(imported, targets, axis=1)], axis=1
        )
        home_sum, other_sum = tile_fn(home_block, partner_fields, usable)
        return (buffer.at[:, targets].add(other_sum[:, 1:]), home_sum)

    initial = jnp.zeros((field_count, imported.shape[1], own_fields.shape[2]), jnp.float32)
    buffer, home_sums = lax.scan(visit, initial, jnp.arange(own_fields.shape[1], dtype=jnp.int32))
    return jnp.moveaxis(home_sums, 0, 1) + return_halves(buffer)


def shards(positions, charges, types, pairs, owner_map):
    intrinsic, offset_rho, scaled_rho = lookup_types(types)
    region_blocks = positions.shape[1] * lax.axis_size("dev")
    region_here = lax.axis_index("region")
    live_slot = pairs >= 0
    partner_ids = owner_map[jnp.maximum(pairs, 0)]
    slot_ids = (
        partner_ids // region_blocks - region_here
    ) * region_blocks + partner_ids % region_blocks
    slot_ids = jnp.where(live_slot, slot_ids, 0)
    first_fields = jnp.concatenate([positions, offset_rho[None], scaled_rho[None]], axis=0)
    first_import = import_fields(first_fields)
    descreen_sum = local_sweep(first_fields, first_import, slot_ids, live_slot, descreen_tile, 1)[0]
    psi_value = descreen_sum * offset_rho
    shaped = (
        born_alpha * psi_value
        - born_beta * psi_value * psi_value
        + born_gamma * psi_value * psi_value * psi_value
    )
    born_radius = 1.0 / (1.0 / offset_rho - jnp.tanh(shaped) / intrinsic)
    second = jnp.concatenate([positions, charges[None], born_radius[None]], axis=0)
    second_import = import_fields(second)
    totals = local_sweep(second, second_import, slot_ids, live_slot, energy_tile, 5)
    charge_sq = solvent_tau * charges * charges
    energy = totals[3] - 0.5 * charge_sq / born_radius
    born_grad = totals[4] + 0.5 * charge_sq / (born_radius * born_radius)
    return (born_radius, energy, totals[:3], born_grad)


def solution(mesh):
    placed = (
        P(None, ("region", "dev"), None),
        P(("region", "dev"), None),
        P(("region", "dev"), None),
        P(("region", "dev"), None),
        P(),
    )
    return jax.shard_map(
        shards,
        mesh=mesh,
        in_specs=placed,
        out_specs=(
            P(("region", "dev"), None),
            P(("region", "dev"), None),
            P(None, ("region", "dev"), None),
            P(("region", "dev"), None),
        ),
        check_vma=False,
    )
```

profile of v0, /device:TPU:1, one launch (start us, length us, event | category | flops | bytes accessed | tf_op | source)
XLA Modules:
  0.0 866.9 jit_solution(13109581444233303802)
XLA Ops:
  8.7 83.4 %all_gather.6 = f32[5,256,128]{2,0,1:T(8,128)S(1)} all-gather(f32[5,4,128]{2,0,1:T(8,128)S(1)} %fusion.14), channel_id=1, replica_groups=mesh['region'=8,'dev'=64] {'dev'}, dimensions={1}, use_global_device_ids=true | all-gather | bytes 665600 | tf_op jit(solution)/shard_map/all_gather | solution.py:121
  92.2 27.6 %collective-permute-start = (f32[5,256,128]{2,1,0:T(8,128)S(1)}, f32[5,256,128]{2,1,0:T(8,128)S(1)}, u32[]{:S(2)}, u32[]{:S(2)}) collective-permute-start(f32[5,256,128]{2,1,0:T(8,128)S(1)} %copy.49), channel_id=1, source_target_pairs={{64,0},{128,64},{192,128},{256,192},{320,256},{384,320},{448,384},... | collective-permute-start | bytes 1966088 | tf_op jit(solution)/shard_map/ppermute | solution.py:18
  120.8 8.3 collective-permute-done
  129.6 1.6 pad_maximum_fusion.3
  131.1 35.5 %while.27 = (s32[]{:T(128)}, f32[1,512,128]{2,1,0:T(8,128)S(1)}, f32[4,1,128]{2,1,0:T(1,128)S(1)}, s32[4]{0:T(128)S(1)}, s32[4,13]{1,0:T(4,128)S(1)}, /*index=5*...) while((s32[]{:T(128)}, f32[1,512,128]{2,1,0:T(8,128)S(1)}, ...), condition=%wide.region_7.12_spmd, body=%wide.region_2.11_spmd.sunk | while | flops 17474200 | bytes 2563646 | solution.py:148
  133.7 2.1 gather_fusion
  136.6 2.6 select_reduce_fusion.16
  142.6 2.1 gather_fusion
  145.5 2.6 select_reduce_fusion.16
  151.5 2.1 gather_fusion
  154.3 2.6 select_reduce_fusion.16
  160.3 2.1 gather_fusion
  163.2 2.6 select_reduce_fusion.16
  166.7 1.9 collective-permute-start.1
  168.6 1.9 collective-permute-done.1
  173.2 249.8 %all-reduce.5.cloned.1.call-done = f32[1,256,128]{2,1,0:T(8,128)} async-done(((f32[1,256,128]{2,1,0:T(8,128)}), f32[1,256,128]{2,1,0:T(8,128)}) %all-reduce.5.cloned.1.call-update) | async-done | bytes 131088
  423.7 73.1 %all_gather.7 = f32[5,256,128]{2,0,1:T(8,128)S(1)} all-gather(f32[5,4,128]{2,0,1:T(8,128)S(1)} %fusion.15), channel_id=1, replica_groups=mesh['region'=8,'dev'=64] {'dev'}, dimensions={1}, use_global_device_ids=true | all-gather | bytes 665600 | tf_op jit(solution)/shard_map/all_gather | solution.py:121
  496.9 37.7 %collective-permute-start.2 = (f32[5,256,128]{2,1,0:T(8,128)S(1)}, f32[5,256,128]{2,1,0:T(8,128)S(1)}, u32[]{:S(2)}, u32[]{:S(2)}) collective-permute-start(f32[5,256,128]{2,1,0:T(8,128)S(1)} %copy.53), channel_id=1, source_target_pairs={{64,0},{128,64},{192,128},{256,192},{320,256},{384,320},{448,384},... | collective-permute-start | bytes 1966088 | tf_op jit(solution)/shard_map/ppermute | solution.py:18
  534.7 9.1 %collective-permute-done.2 = f32[5,256,128]{2,1,0:T(8,128)S(1)} collective-permute-done((f32[5,256,128]{2,1,0:T(8,128)S(1)}, f32[5,256,128]{2,1,0:T(8,128)S(1)}, u32[]{:S(2)}, u32[]{:S(2)}) %collective-permute-start.2) | collective-permute-done | bytes 655392 | tf_op jit(solution)/shard_map/ppermute | solution.py:18
  544.2 1.6 pad_maximum_fusion.4
  545.9 44.7 %while.28 = (s32[]{:T(128)}, f32[5,512,128]{2,0,1:T(8,128)S(1)}, f32[4,5,128]{2,0,1:T(4,128)S(1)}, s32[4]{0:T(128)S(1)}, s32[4,13]{1,0:T(4,128)S(1)}, /*index=5*...) while((s32[]{:T(128)}, f32[5,512,128]{2,0,1:T(8,128)S(1)}, ...), condition=%wide.region_22.27_spmd, body=%wide.region_9.26_spmd.sunk | while | flops 17467544 | bytes 12730510 | solution.py:148
  548.5 2.1 gather_fusion.1
  552.7 3.2 select_reduce_fusion.17
  559.7 2.1 gather_fusion.1
  563.9 3.2 select_reduce_fusion.17
  570.8 2.1 gather_fusion.1
  575.1 3.2 select_reduce_fusion.17
  582.0 2.1 gather_fusion.1
  586.2 3.2 select_reduce_fusion.17
  590.9 1.9 collective-permute-start.3
  592.8 7.5 collective-permute-done.3
  601.3 255.5 %all-reduce.7.cloned.1.call-done = f32[5,256,128]{2,1,0:T(8,128)} async-done(((f32[5,256,128]{2,1,0:T(8,128)}), f32[5,256,128]{2,1,0:T(8,128)}) %all-reduce.7.cloned.1.call-update) | async-done | bytes 655376
  (242 shorter events, 33.8 us)
Async XLA Ops:
  7.2 112.8 %copy-start = (s32[2048]{0:T(1024)S(1)}, s32[2048]{0:T(1024)}, u32[]{:S(2)}) copy-start(s32[2048]{0:T(1024)} %param.23) | copy-start | bytes 24580
  7.2 112.6 %copy-start.2 = (s32[4,13]{1,0:T(4,128)S(1)}, s32[4,13]{1,0:T(4,128)}, u32[]{:S(2)}) copy-start(s32[4,13]{1,0:T(4,128)} %param.22) | copy-start | bytes 628
  7.2 415.8 %all-reduce.5.cloned.1.call-start = ((), (), s32[]{:S(2)}) async-start(), calls=%async_computation | async-start | bytes 262144
  92.2 36.9 %collective-permute-start = (f32[5,256,128]{2,1,0:T(8,128)S(1)}, f32[5,256,128]{2,1,0:T(8,128)S(1)}, u32[]{:S(2)}, u32[]{:S(2)}) collective-permute-start(f32[5,256,128]{2,1,0:T(8,128)S(1)} %copy.49), channel_id=1, source_target_pairs={{64,0},{128,64},{192,128},{256,192},{320,256},{384,320},{448,384},... | collective-permute-start | bytes 1966088 | tf_op jit(solution)/shard_map/ppermute | solution.py:18
  131.1 292.5 %copy-start.1 = (f32[4,128]{1,0:T(4,128)S(1)}, f32[4,128]{1,0:T(4,128)}, u32[]{:S(2)}) copy-start(f32[4,128]{1,0:T(4,128)} %param.20) | copy-start | bytes 6148
  166.7 3.9 collective-permute-start.1
  171.2 685.6 %all-reduce.7.cloned.1.call-start = ((), (), s32[]{:S(2)}) async-start(), calls=%async_computation.1 | async-start | bytes 1310720
  496.9 46.9 %collective-permute-start.2 = (f32[5,256,128]{2,1,0:T(8,128)S(1)}, f32[5,256,128]{2,1,0:T(8,128)S(1)}, u32[]{:S(2)}, u32[]{:S(2)}) collective-permute-start(f32[5,256,128]{2,1,0:T(8,128)S(1)} %copy.53), channel_id=1, source_target_pairs={{64,0},{128,64},{192,128},{256,192},{320,256},{384,320},{448,384},... | collective-permute-start | bytes 1966088 | tf_op jit(solution)/shard_map/ppermute | solution.py:18
  590.9 9.4 %collective-permute-start.3 = (f32[5,256,128]{2,1,0:T(8,128)S(1)}, f32[5,256,128]{2,1,0:T(8,128)S(1)}, u32[]{:S(2)}, u32[]{:S(2)}) collective-permute-start(f32[5,256,128]{2,1,0:T(8,128)S(1)} %slice.123), channel_id=1, source_target_pairs={{0,64},{64,128},{128,192},{192,256},{256,320},{320,384},{384,448},... | collective-permute-start | bytes 1966088 | tf_op jit(solution)/shard_map/ppermute | solution.py:18
Sparse Core Ops, SparseCore 0:
  171.3 251.5 all-reduce.4
  601.5 255.2 all-reduce.6
where the time goes:
time: 877 us; the launch traced here: 867 us
  waiting for transfers between devices  532 us (61%)
  blocking collectives  156 us (18%)
  starting transfers between devices  69.2 us (8%)
  other arithmetic  49.6 us (6%)
  local copies, waits for them, and re-layouts  27.5 us (3%)
  loops' own time  17 us (2%)
  between operations  14.9 us (2%)
    unnamed x4, waiting for transfers between devices  505 us
    all_gather x2, blocking collectives, import_fields(): home_slab = lax.all_gather(payload, 'dev', axis=1, tiled=True)  156 us
    ppermute x4, starting transfers between devices, passed_along(): return lax.ppermute(value, axis, pairs)  69.1 us
    ppermute x4, waiting for transfers between devices, passed_along(): return lax.ppermute(value, axis, pairs)  26.9 us
    reduce_sum x8, other arithmetic, masked_sum(): return jnp.sum(jnp.where(keep_mask, values, 0.0), axis=reduce_axes)  23.1 us
  transfers between devices with their start and end apart: 6, of which 6 were waited for; matrix products, arithmetic and copies ran while one was open for 0% of the time, Pallas kernels for 0%

commit v1 on v0

v1 whole, which is shorter than its diff:
```python
import functools
import math

import jax
import jax.numpy as jnp
from jax import lax
from jax.experimental import pallas as pl
from jax.experimental.pallas import tpu as pltpu
from jax.sharding import PartitionSpec as P

type_radii = (1.2, 1.7, 1.55, 1.52, 1.85, 1.8)
type_scales = (0.85, 0.72, 0.79, 0.85, 0.86, 0.96)
radius_offset = 0.09
born_alpha = 1.0
born_beta = 0.8
born_gamma = 4.85
solvent_tau = 1.0 - 1.0 / 78.5

MESH = pl.DeviceIdType.MESH
NREG = 8
NZ = 16
NY = 4
NDEV = NZ * NY
BLK = 4
SLOTS = 13
ATOMS = 128
ROWS1 = 24
ROWS2 = 8
REGION_BLOCKS = NDEV * BLK
REV = 32
LIST = 64
F32 = jnp.float32
I32 = jnp.int32
HIGH = lax.Precision.HIGHEST
NT = (((1,), (1,)), ((), ()))


def table(types, values):
    out = jnp.full(types.shape, values[0], F32)
    for i in range(1, len(values)):
        out = jnp.where(types == i, F32(values[i]), out)
    return out


def pack_kernel(pairs, pos, types, out):
    for f in range(3):
        out[4 * f : 4 * f + 4, :] = pos[f]
    kinds = types[...]
    rho = table(kinds, type_radii) - radius_offset
    out[12:16, :] = rho
    out[16:20, :] = table(kinds, type_scales) * rho
    lane = lax.broadcasted_iota(I32, (1, ATOMS), 1)
    row = jnp.full((1, ATOMS), -1, I32)
    for b in range(BLK):
        for k in range(SLOTS):
            row = jnp.where(lane == b * SLOTS + k, pairs[b, k], row)
    out[20:21, :] = row.astype(F32)
    out[21:24, :] = jnp.zeros((3, ATOMS), F32)


def pack(positions, types, pairs):
    return pl.pallas_call(
        pack_kernel,
        out_shape=jax.ShapeDtypeStruct((ROWS1, ATOMS), F32),
        in_specs=[
            pl.BlockSpec(memory_space=pltpu.SMEM),
            pl.BlockSpec(memory_space=pltpu.VMEM),
            pl.BlockSpec(memory_space=pltpu.VMEM),
        ],
        out_specs=pl.BlockSpec(memory_space=pltpu.VMEM),
        name="pack",
    )(pairs, positions, types)


def gather_kernel(x, out, local, ysend, yrecv, zsend, zrecv, fsend, frecv):
    r = lax.axis_index("region")
    d = lax.axis_index("dev")
    z = d // NY
    y = d % NY
    odd = r % 2
    sibling = r + 1 - 2 * odd
    beside = (r + 2 * odd - 1 + NREG) % NREG
    up = (z + 1) % NZ
    down = (z + NZ - 1) % NZ

    peers = [(r, z * NY + (y + k) % NY) for k in range(1, NY)]
    peers += [(r, up * NY + y), (r, down * NY + y), (sibling, d), (beside, d)]
    barrier = pltpu.get_barrier_semaphore()
    for peer in peers:
        pl.semaphore_signal(barrier, inc=1, device_id=peer, device_id_type=MESH)
    own = pltpu.make_async_copy(x, out.at[d], local)
    own.start()
    pl.semaphore_wait(barrier, len(peers))

    sends = []

    def send(src, dst, ssem, rsem, to):
        copy = pltpu.make_async_remote_copy(
            src_ref=src, dst_ref=dst, send_sem=ssem, recv_sem=rsem, device_id=to, device_id_type=MESH
        )
        copy.start()
        sends.append(copy)

    def wait_for(dst, rsem):
        pltpu.make_async_remote_copy(
            src_ref=dst, dst_ref=dst, send_sem=rsem, recv_sem=rsem, device_id=(sibling, d), device_id_type=MESH
        ).wait_recv()

    def column(slot, zz):
        return out.at[pl.ds(slot * NDEV + zz * NY, NY)]

    for k in range(1, NY):
        send(x, out.at[d], ysend.at[k - 1], yrecv.at[k - 1], (r, z * NY + (y + k) % NY))
    own.wait()
    for k in range(1, NY):
        wait_for(out.at[z * NY + (y + NY - k) % NY], yrecv.at[k - 1])

    def forward(zz, n):
        send(column(0, zz), column(2, zz), fsend.at[1, n], frecv.at[1, n], (beside, d))
        send(column(0, zz), column(1, zz), fsend.at[0, n], frecv.at[0, n], (sibling, d))

    half = NZ // 2
    for s in range(1, half + 1):
        behind = (z + NZ - (s - 1)) % NZ
        ahead = (z + (s - 1)) % NZ
        send(column(0, behind), column(0, behind), zsend.at[0, s - 1], zrecv.at[0, s - 1], (r, up * NY + y))
        if s < half:
            send(column(0, ahead), column(0, ahead), zsend.at[1, s - 1], zrecv.at[1, s - 1], (r, down * NY + y))
        forward(behind, s - 1)
        if s > 1:
            forward(ahead, half + s - 1)
        wait_for(column(0, (z + NZ - s) % NZ), zrecv.at[0, s - 1])
        if s < half:
            wait_for(column(0, (z + s) % NZ), zrecv.at[1, s - 1])
    forward((z + half) % NZ, half)

    for n in range(NZ):
        zz = (z + NZ - n) % NZ if n <= half else (z + n - half) % NZ
        wait_for(column(1, zz), frecv.at[0, n])
        wait_for(column(2, zz), frecv.at[1, n])
    for copy in sends:
        copy.wait_send()


def gather(payload, rows, ident):
    dma = pltpu.SemaphoreType.DMA
    return pl.pallas_call(
        gather_kernel,
        out_shape=jax.ShapeDtypeStruct((3 * NDEV, rows, ATOMS), F32),
        in_specs=[pl.BlockSpec(memory_space=pltpu.VMEM)],
        out_specs=pl.BlockSpec(memory_space=pltpu.VMEM),
        scratch_shapes=[
            dma,
            dma((NY - 1,)),
            dma((NY - 1,)),
            dma((2, NZ // 2)),
            dma((2, NZ // 2)),
            dma((2, NZ)),
            dma((2, NZ)),
        ],
        compiler_params=pltpu.CompilerParams(collective_id=ident, has_side_effects=True),
        name="gather%d" % ident,
    )(payload)


def ids_here():
    return lax.axis_index("region"), lax.axis_index("dev")


def spread(columns, ref):
    turned = jnp.transpose(columns)
    for f in range(ref.shape[0]):
        ref[f] = jnp.broadcast_to(turned[:, f : f + 1], (ATOMS, ATOMS))


def row_sums(values):
    return lax.dot_general(jnp.ones((8, ATOMS), F32), values, NT, precision=HIGH, preferred_element_type=F32)[0:1]


def h_term(r2, a, ia2, s):
    ir = lax.rsqrt(r2)
    r = r2 * ir
    upper = r + s
    gap = r - s
    lower = jnp.maximum(a, jnp.abs(gap))
    il = 1.0 / lower
    iu = 1.0 / upper
    dif = il - iu
    tot = il + iu
    bent = 0.25 * (s * s * ir - r)
    value = dif + dif * tot * bent + (0.5 * math.log(2.0)) * ir * jnp.log2(lower * iu)
    value = value + jnp.where(gap < -a, ia2 - (il + il), 0.0)
    return jnp.where(upper > a, value, 0.0)


def find_partners(r, d, pairs, owners_s, owners, fields, lst, cnt, found, found_s, sem):
    odd = r % 2
    previous = 2 - odd
    base = r * REGION_BLOCKS + d * BLK
    ids = lax.broadcasted_iota(I32, (16, ATOMS), 0) * ATOMS + lax.broadcasted_iota(I32, (16, ATOMS), 1)
    held = owners[...]
    listed = jnp.concatenate(
        [
            fields[pl.ds(20, NDEV, stride=ROWS1), :],
            fields[pl.ds(previous * NDEV * ROWS1 + 20, NDEV, stride=ROWS1), :],
        ],
        axis=0,
    )
    sub = lax.broadcasted_iota(I32, (16, ATOMS), 0)
    lane = lax.broadcasted_iota(I32, (16, ATOMS), 1)
    hits = jnp.zeros((16, ATOMS), F32)
    for b in range(BLK):
        cell = jnp.sum(jnp.where(held == base + b, ids, 0).astype(F32))
        match = (listed == cell).astype(F32)
        pick = ((sub // BLK == b) & (lane // SLOTS == sub % BLK)).astype(F32)
        hits = hits + lax.dot_general(pick, match, NT, preferred_element_type=F32)
    row = lax.broadcasted_iota(I32, (ATOMS, ATOMS), 0)
    col = lax.broadcasted_iota(I32, (ATOMS, ATOMS), 1)
    prefix = (row <= col).astype(F32)
    s0 = lax.broadcasted_iota(I32, (16, 16), 0)
    s1 = lax.broadcasted_iota(I32, (16, 16), 1)
    before = ((s0 // BLK == s1 // BLK) & (s1 < s0)).astype(F32)
    rank = jnp.dot(hits, prefix, preferred_element_type=F32)
    earlier = jnp.dot(before, hits, preferred_element_type=F32)
    rank = rank + jnp.dot(earlier, jnp.ones((ATOMS, ATOMS), F32), preferred_element_type=F32)
    rank = jnp.where(hits > 0.5, rank, 0.0)
    wanted = (lax.broadcasted_iota(I32, (REV, ATOMS), 0) + 1).astype(F32)
    slot_dev = lax.broadcasted_iota(I32, (1, ATOMS), 1)
    slot_dev = jnp.where(slot_dev < NDEV, slot_dev, slot_dev + (previous - 1) * NDEV)
    picked = []
    for b in range(BLK):
        total = jnp.zeros((REV, ATOMS), F32)
        for o in range(BLK):
            code = (slot_dev * BLK + o + 1).astype(F32)
            total = total + jnp.where(rank[b * BLK + o : b * BLK + o + 1] == wanted, code, 0.0)
        picked.append(total)
    picked = jnp.concatenate(picked, axis=0)
    codes = lax.dot_general(jnp.ones((8, ATOMS), F32), picked, NT, precision=HIGH, preferred_element_type=F32)
    found[...] = (codes + 0.5).astype(I32)
    copy = pltpu.make_async_copy(found, found_s, sem)
    copy.start()
    for b in range(BLK):

        def listing(k, n, b=b):
            cell = pairs[b, k]
            partner = owners_s[jnp.maximum(cell, 0)]
            region = partner // REGION_BLOCKS
            slot = jnp.where(region == r, 0, jnp.where(region == r + 1 - 2 * odd, 1, 2))
            lst[b, n] = slot * REGION_BLOCKS + partner % REGION_BLOCKS
            return n + (cell >= 0).astype(I32)

        cnt[b] = lax.fori_loop(0, SLOTS, listing, jnp.int32(0), unroll=True)
    copy.wait()
    for b in range(BLK):

        def reverse(k, n, b=b):
            code = found_s[0, b * REV + k]
            lst[b, n] = code - 1
            return n + (code > 0).astype(I32)

        cnt[b] = lax.fori_loop(0, REV, reverse, cnt[b], unroll=8)


CHUNK1 = 64
CHUNK2 = 32


def fetch(ref, start):
    return ref[pl.ds(start, 1), :]


def descreen_kernel(
    where, pairs, owners_s, owners, types, charges, fields, out, lst, cnt, home, acc, found, found_s, sem
):
    r, d = where()
    find_partners(r, d, pairs, owners_s, owners, fields, lst, cnt, found, found_s, sem)
    sums = []
    for b in range(BLK):
        own = d * ROWS1 + b
        rho_row = fetch(fields, own + 12)
        rows = [fetch(fields, own), fetch(fields, own + 4), fetch(fields, own + 8), rho_row, 2.0 / rho_row]
        spread(jnp.concatenate(rows + [jnp.zeros((3, ATOMS), F32)], axis=0), home)

        def chunk(c, carry, b=b, own=own):
            span = pl.ds(pl.multiple_of(c * CHUNK1, CHUNK1), CHUNK1)
            hx, hy, hz, ha, hi = (home[f, span, :] for f in range(5))

            def tile(start, mask=None):
                dx = hx - fetch(fields, start)
                dy = hy - fetch(fields, start + 4)
                dz = hz - fetch(fields, start + 8)
                r2 = dx * dx + dy * dy + dz * dz
                if mask is not None:
                    r2 = jnp.where(mask, 1.0, r2)
                return h_term(r2, ha, hi, fetch(fields, start + 16))

            diagonal = lax.broadcasted_iota(I32, (CHUNK1, ATOMS), 1) == (
                lax.broadcasted_iota(I32, (CHUNK1, ATOMS), 0) + c * CHUNK1
            )
            total = jnp.where(diagonal, 0.0, tile(own, diagonal))

            def step(n, total):
                e = lst[b, n]
                return total + tile((e // BLK) * ROWS1 + e % BLK)

            acc[span, :] = lax.fori_loop(0, cnt[b], step, total)
            return carry

        lax.fori_loop(0, ATOMS // CHUNK1, chunk, 0)
        sums.append(row_sums(acc[...]))
    descreen = 0.5 * jnp.concatenate(sums, axis=0)
    rho0 = table(types[...], type_radii)
    rho = rho0 - radius_offset
    psi = descreen * rho
    shaped = born_alpha * psi - born_beta * psi * psi + born_gamma * psi * psi * psi
    out[0:4, :] = 1.0 / (1.0 / rho - jnp.tanh(shaped) / rho0)
    out[4:8, :] = charges[...]


def descreen_stage(where, pairs, owner_map, types, charges, fields):
    smem = pl.BlockSpec(memory_space=pltpu.SMEM)
    vmem = pl.BlockSpec(memory_space=pltpu.VMEM)
    return pl.pallas_call(
        functools.partial(descreen_kernel, where),
        out_shape=(
            jax.ShapeDtypeStruct((ROWS2, ATOMS), F32),
            jax.ShapeDtypeStruct((BLK, LIST), I32),
            jax.ShapeDtypeStruct((BLK,), I32),
        ),
        in_specs=[smem, smem, vmem, vmem, vmem, vmem],
        out_specs=(vmem, smem, smem),
        scratch_shapes=[
            pltpu.VMEM((5, ATOMS, ATOMS), F32),
            pltpu.VMEM((ATOMS, ATOMS), F32),
            pltpu.VMEM((8, ATOMS), I32),
            pltpu.SMEM((8, ATOMS), I32),
            pltpu.SemaphoreType.DMA,
        ],
        name="descreen",
    )(pairs, owner_map, owner_map.reshape(16, ATOMS), types, charges, fields.reshape(-1, ATOMS))


def energy_kernel(where, lst, cnt, fields, radii, energy, forces, grad, home, acc):
    r, d = where()
    for b in range(BLK):
        own = d * ROWS1 + b
        own2 = d * ROWS2 + b
        radius = fetch(radii, own2)
        charge = fetch(radii, own2 + 4)
        inverse = 1.0 / radius
        rows = [fetch(fields, own), fetch(fields, own + 4), fetch(fields, own + 8), solvent_tau * charge, radius]
        rows.append((-0.25 * math.log2(math.e)) * inverse)
        spread(jnp.concatenate(rows + [jnp.zeros((2, ATOMS), F32)], axis=0), home)

        def chunk(c, carry, b=b, own=own, own2=own2):
            span = pl.ds(pl.multiple_of(c * CHUNK2, CHUNK2), CHUNK2)
            hx, hy, hz, hq, hr, hd = (home[f, span, :] for f in range(6))

            def tile(start, start2, totals, mask=None):
                dx = hx - fetch(fields, start)
                dy = hy - fetch(fields, start + 4)
                dz = hz - fetch(fields, start + 8)
                radius_j = fetch(radii, start2)
                charge_j = fetch(radii, start2 + 4)
                r2 = dx * dx + dy * dy + dz * dz
                if mask is not None:
                    r2 = jnp.where(mask, 1.0, r2)
                arg = r2 * (hd * (1.0 / radius_j))
                damped = jnp.exp2(arg)
                inv = lax.rsqrt(r2 + hr * radius_j * damped)
                e = hq * charge_j * inv
                if mask is not None:
                    e = jnp.where(mask, 0.0, e)
                e3 = e * (inv * inv)
                e3d = e3 * damped
                pull = e3 - 0.25 * e3d
                g = (e3d * radius_j) * (1.0 - math.log(2.0) * arg)
                fx, fy, fz, te, tg = totals
                return (fx + pull * dx, fy + pull * dy, fz + pull * dz, te + e, tg + g)

            diagonal = lax.broadcasted_iota(I32, (CHUNK2, ATOMS), 1) == (
                lax.broadcasted_iota(I32, (CHUNK2, ATOMS), 0) + c * CHUNK2
            )
            totals = (jnp.zeros((CHUNK2, ATOMS), F32),) * 5
            totals = tile(own, own2, totals, diagonal)

            def step(n, totals):
                e = lst[b, n]
                dev = e // BLK
                blk = e % BLK
                return tile(dev * ROWS1 + blk, dev * ROWS2 + blk, totals)

            totals = lax.fori_loop(0, cnt[b], step, totals)
            for f in range(5):
                acc[f, span, :] = totals[f]
            return carry

        lax.fori_loop(0, ATOMS // CHUNK2, chunk, 0)
        for f in range(3):
            forces[f, b : b + 1, :] = -row_sums(acc[f])
        self_e = solvent_tau * charge * charge
        energy[b : b + 1, :] = -0.5 * row_sums(acc[3]) - 0.5 * self_e * inverse
        grad[b : b + 1, :] = 0.5 * row_sums(acc[4]) + 0.5 * self_e * inverse * inverse


def energy_stage(where, lst, cnt, fields, radii):
    smem = pl.BlockSpec(memory_space=pltpu.SMEM)
    vmem = pl.BlockSpec(memory_space=pltpu.VMEM)
    return pl.pallas_call(
        functools.partial(energy_kernel, where),
        out_shape=(
            jax.ShapeDtypeStruct((BLK, ATOMS), F32),
            jax.ShapeDtypeStruct((3, BLK, ATOMS), F32),
            jax.ShapeDtypeStruct((BLK, ATOMS), F32),
        ),
        in_specs=[smem, smem, vmem, vmem],
        out_specs=(vmem, vmem, vmem),
        scratch_shapes=[pltpu.VMEM((6, ATOMS, ATOMS), F32), pltpu.VMEM((5, ATOMS, ATOMS), F32)],
        name="energy",
    )(lst, cnt, fields.reshape(-1, ATOMS), radii.reshape(-1, ATOMS))


def shards(positions, charges, types, pairs, owner_map):
    fields = gather(pack(positions, types, pairs), ROWS1, 0)
    mine, lst, cnt = descreen_stage(ids_here, pairs, owner_map, types, charges, fields)
    radii = gather(mine, ROWS2, 1)
    energy, forces, grad = energy_stage(ids_here, lst, cnt, fields, radii)
    return (mine[:BLK], energy, forces, grad)


def solution(mesh):
    placed = (
        P(None, ("region", "dev"), None),
        P(("region", "dev"), None),
        P(("region", "dev"), None),
        P(("region", "dev"), None),
        P(),
    )
    return jax.shard_map(
        shards,
        mesh=mesh,
        in_specs=placed,
        out_specs=(
            P(("region", "dev"), None),
            P(("region", "dev"), None),
            P(None, ("region", "dev"), None),
            P(("region", "dev"), None),
        ),
        check_vma=False,
    )
```

time: 877 us -> 134 us (0.15)
  the two profiles are of different devices: /device:TPU:1 before, /device:TPU:13 now
where the time goes in v1:
time: 134 us; the launch traced here: 133 us
  Pallas kernels  131 us (98%)
    pallas_call x2, Pallas kernels, gather(): pl.pallas_call(gather_kernel, out_shape=jax.ShapeDtypeStruct((3 * NDEV, r...  85.9 us
    pallas_call x1, Pallas kernels, energy_stage(): pl.pallas_call(functools.partial(energy_kernel, where), out_shape=(jax.Sh...  24.8 us
    pallas_call x1, Pallas kernels, descreen_stage(): pl.pallas_call(functools.partial(descreen_kernel, where), out_shape=(jax....  19.2 us

profile of v1, /device:TPU:13, one launch (start us, length us, event | category | flops | bytes accessed | tf_op | source)
XLA Modules:
  0.0 133.2 jit_solution(6120245230741037320)
XLA Ops:
  0.6 1.3 %pack.1.x = f32[24,128]{1,0:T(8,128)} custom-call(s32[4,13]{1,0:T(4,128)} %pairs.3, f32[3,4,128]{2,1,0:T(4,128)} %pos.1, s32[4,128]{1,0:T(4,128)} %types.3), custom_call_target="tpu_custom_call" | custom-call | tf_op jit(solution)/shard_map/pack/pallas_call | solution.py:62
  2.0 50.4 %gather0.1 = f32[192,24,128]{2,1,0:T(8,128)} custom-call(f32[24,128]{1,0:T(8,128)} %pack.1.x), custom_call_target="tpu_custom_call" | custom-call | tf_op jit(solution)/shard_map/gather0/pallas_call | solution.py:147
  52.4 19.2 %descreen.1 = (f32[8,128]{1,0:T(8,128)}, s32[4,64]{1,0:T(4,128)}, s32[4]{0:T(128)}) custom-call(s32[4,13]{1,0:T(4,128)} %pairs.3, s32[2048]{0:T(1024)} %owners_s.1, s32[16,128]{1,0:T(8,128)} %bitcast.6, s32[4,128]{1,0:T(4,128)} %types.3, f32[4,128]{1,0:T(4,128)} %charges.1, f32[4608,128]{1,0:T(8,128)} %bitcast.3), custom_call_target="tpu_custom_call" | custom-call | tf_op jit(solution)/shard_map/descreen/pallas_call | solution.py:323
  71.5 1.3 slice.3
  72.8 35.5 %gather1.1 = f32[192,8,128]{2,1,0:T(8,128)} custom-call(f32[8,128]{1,0:T(8,128)} %get-tuple-element.10.x), custom_call_target="tpu_custom_call" | custom-call | tf_op jit(solution)/shard_map/gather1/pallas_call | solution.py:147
  108.3 24.8 %energy.1 = (f32[4,128]{1,0:T(4,128)}, f32[3,4,128]{2,1,0:T(4,128)}, f32[4,128]{1,0:T(4,128)}) custom-call(s32[4,64]{1,0:T(4,128)} %get-tuple-element.11.lst, s32[4]{0:T(128)} %get-tuple-element.12.cnt, f32[4608,128]{1,0:T(8,128)} %bitcast.4, f32[1536,128]{1,0:T(8,128)} %bitcast.5), custom_call_target="tpu_custom_call" | custom-call | tf_op jit(solution)/shard_map/energy/pallas_call | solution.py:409

commit v2 on v1

v2 whole, which is shorter than its diff:
```python
import functools
import math

import jax
import jax.numpy as jnp
from jax import lax
from jax.experimental import pallas as pl
from jax.experimental.pallas import tpu as pltpu
from jax.sharding import PartitionSpec as P

type_radii = (1.2, 1.7, 1.55, 1.52, 1.85, 1.8)
type_scales = (0.85, 0.72, 0.79, 0.85, 0.86, 0.96)
radius_offset = 0.09
born_alpha = 1.0
born_beta = 0.8
born_gamma = 4.85
solvent_tau = 1.0 - 1.0 / 78.5

MESH = pl.DeviceIdType.MESH
NREG = 8
NZ = 16
NY = 4
NDEV = NZ * NY
BLK = 4
SLOTS = 13
ATOMS = 128
ROWS1 = 17
ROWS2 = 8
REGION_BLOCKS = NDEV * BLK
REV = 32
LIST = 64
HALF = NZ // 2
REACH = 4
PIECES = ((4, 13), (0, 4), (13, 16))
F32 = jnp.float32
I32 = jnp.int32
HIGH = lax.Precision.HIGHEST
NT = (((1,), (1,)), ((), ()))


def table(types, values):
    out = jnp.full(types.shape, values[0], F32)
    for i in range(1, len(values)):
        out = jnp.where(types == i, F32(values[i]), out)
    return out


def gather_body(fill, x, out, local, zsend, zrecv, ysend, yrecv, fsend, frecv):
    r = lax.axis_index("region")
    d = lax.axis_index("dev")
    z = d // NY
    y = d % NY
    odd = r % 2
    sibling = (r + 1 - 2 * odd, d)
    beside = ((r + 2 * odd - 1 + NREG) % NREG, d)

    def zpeer(k):
        return (r, (z + k + NZ) % NZ * NY + y)

    hops = sorted((k for k in range(-REACH, REACH + 1) if k), key=abs)
    ypeers = [(r, z * NY + (y + k) % NY) for k in range(1, NY)]
    everyone = [zpeer(k) for k in hops] + ypeers + [sibling, beside]
    barrier = pltpu.get_barrier_semaphore()
    for peer in everyone:
        pl.semaphore_signal(barrier, inc=1, device_id=peer, device_id_type=MESH)
    fill()
    pl.semaphore_wait(barrier, len(everyone))
    mine = out.at[0, y, HALF]
    own = pltpu.make_async_copy(x, mine, local)
    own.start()
    own.wait()
    sends = []

    def send(src, dst, ssem, rsem, to):
        copy = pltpu.make_async_remote_copy(
            src_ref=src, dst_ref=dst, send_sem=ssem, recv_sem=rsem, device_id=to, device_id_type=MESH
        )
        copy.start()
        sends.append(copy)

    def wait_for(dst, rsem):
        pltpu.make_async_remote_copy(
            src_ref=dst, dst_ref=dst, send_sem=rsem, recv_sem=rsem, device_id=sibling, device_id_type=MESH
        ).wait_recv()

    def part(slot, yy, a, b):
        return out.at[slot, yy, pl.ds(a, b - a)]

    for n, k in enumerate(hops):
        send(mine, out.at[0, y, HALF - k], zsend.at[n], zrecv.at[HALF - k], zpeer(k))

    def forward(yy, k, p):
        span = PIECES[p]
        send(part(0, yy, *span), part(2, yy, *span), fsend.at[1, k, p], frecv.at[1, k, p], beside)
        send(part(0, yy, *span), part(1, yy, *span), fsend.at[0, k, p], frecv.at[0, k, p], sibling)

    low, high = HALF - REACH, HALF + REACH + 1
    for p, span in enumerate(PIECES):
        if p == 0:
            for k in hops:
                wait_for(out.at[0, y, HALF + k], zrecv.at[HALF + k])
            send(part(0, y, low, HALF), part(0, y, 0, low), zsend.at[2 * REACH], zrecv.at[0], zpeer(REACH))
            send(
                part(0, y, HALF + 1, HALF + REACH),
                part(0, y, high, NZ),
                zsend.at[2 * REACH + 1],
                zrecv.at[high],
                zpeer(-REACH),
            )
        else:
            wait_for(part(0, y, *span), zrecv.at[span[0]])
        for k in (2, 1, 3):
            send(part(0, y, *span), part(0, y, *span), ysend.at[k - 1, p], yrecv.at[k - 1, p], ypeers[k - 1])
        forward(y, 0, p)
        for q in [p - 1] * (p > 0) + [p] * (p == len(PIECES) - 1):
            for k in (1, 3, 2):
                yy = (y + NY - k) % NY
                wait_for(part(0, yy, *PIECES[q]), yrecv.at[k - 1, q])
                forward(yy, k, q)
    for p, span in enumerate(PIECES):
        for k in range(NY):
            yy = (y + NY - k) % NY
            wait_for(part(1, yy, *span), frecv.at[0, k, p])
            wait_for(part(2, yy, *span), frecv.at[1, k, p])
    for copy in sends:
        copy.wait_send()


def gather_scratch():
    dma = pltpu.SemaphoreType.DMA
    parts = len(PIECES)
    return [
        dma,
        dma((NZ,)),
        dma((NZ,)),
        dma((NY - 1, parts)),
        dma((NY - 1, parts)),
        dma((2, NY, parts)),
        dma((2, NY, parts)),
    ]


def fields_kernel(pairs, pos, types, out, x, *sems):
    def fill():
        for b in range(BLK):
            for f in range(3):
                x[4 * f + b, :, :] = pos[f, b : b + 1, :]
            x[12 + b, :, :] = types[b : b + 1, :].astype(F32)
        lane = lax.broadcasted_iota(I32, (1, ATOMS), 1)
        row = jnp.full((1, ATOMS), -1, I32)
        for b in range(BLK):
            for k in range(SLOTS):
                row = jnp.where(lane == b * SLOTS + k, pairs[b, k], row)
        x[16, :, :] = row.astype(F32)

    gather_body(fill, x, out, *sems)


def gather_fields(positions, types, pairs):
    vmem = pl.BlockSpec(memory_space=pltpu.VMEM)
    return pl.pallas_call(
        fields_kernel,
        out_shape=jax.ShapeDtypeStruct((3, NY, NZ, ROWS1, 1, ATOMS), F32),
        in_specs=[pl.BlockSpec(memory_space=pltpu.SMEM), vmem, vmem],
        out_specs=vmem,
        scratch_shapes=[pltpu.VMEM((ROWS1, 1, ATOMS), F32)] + gather_scratch(),
        compiler_params=pltpu.CompilerParams(collective_id=0, has_side_effects=True),
        name="gather_fields",
    )(pairs, positions, types)


def radii_kernel(x, out, *sems):
    gather_body(lambda: None, x, out, *sems)


def gather_radii(payload):
    vmem = pl.BlockSpec(memory_space=pltpu.VMEM)
    return pl.pallas_call(
        radii_kernel,
        out_shape=jax.ShapeDtypeStruct((3, NY, NZ, ROWS2, ATOMS), F32),
        in_specs=[vmem],
        out_specs=vmem,
        scratch_shapes=gather_scratch(),
        compiler_params=pltpu.CompilerParams(collective_id=1, has_side_effects=True),
        name="gather_radii",
    )(payload)


def ids_here():
    return lax.axis_index("region"), lax.axis_index("dev")


def own_place(d):
    return (d & (NY - 1)) * NZ + HALF


def spread(columns, ref):
    turned = jnp.transpose(columns)
    for f in range(ref.shape[0]):
        ref[f] = jnp.broadcast_to(turned[:, f : f + 1], (ATOMS, ATOMS))


def row_sums(values):
    return lax.dot_general(jnp.ones((8, ATOMS), F32), values, NT, precision=HIGH, preferred_element_type=F32)[0:1]


def h_term(r2, a, ia8, s):
    ir = lax.rsqrt(r2)
    r = r2 * ir
    upper = r + s
    gap = s - r
    lower = jnp.maximum(a, jnp.abs(gap))
    il = 1.0 / lower
    iu = 1.0 / upper
    value = (il - iu) * (4.0 + (il + iu) * (s * s * ir - r)) + (ir + ir) * jnp.log(lower * iu)
    value = value + jnp.where(a < gap, ia8 - 8.0 * il, 0.0)
    return jnp.where(upper > a, value, 0.0)


def find_partners(r, d, pairs, owners_s, owners, fields, lst1, lst2, cnt, listed, found, found_s, sem):
    odd = r & 1
    previous = 2 - odd
    base = r * REGION_BLOCKS + d * BLK
    ids = lax.broadcasted_iota(I32, (16, ATOMS), 0) * ATOMS + lax.broadcasted_iota(I32, (16, ATOMS), 1)
    held = owners[...]
    for half, place in enumerate((0, previous * NDEV)):

        def take(n, carry, half=half, place=place):
            listed[pl.ds(half * NDEV + n, 1), :] = fields[(place + n) * ROWS1 + 16]
            return carry

        lax.fori_loop(0, NDEV, take, 0, unroll=16)
    known = listed[...]
    sub = lax.broadcasted_iota(I32, (16, ATOMS), 0)
    lane = lax.broadcasted_iota(I32, (16, ATOMS), 1)
    hits = jnp.zeros((16, ATOMS), F32)
    for b in range(BLK):
        cell = jnp.sum(jnp.where(held == base + b, ids, 0).astype(F32))
        match = (known == cell).astype(F32)
        first = (sub & 3) * SLOTS
        pick = (((sub >> 2) == b) & (lane >= first) & (lane < first + SLOTS)).astype(F32)
        hits = hits + lax.dot_general(pick, match, NT, preferred_element_type=F32)
    row = lax.broadcasted_iota(I32, (ATOMS, ATOMS), 0)
    col = lax.broadcasted_iota(I32, (ATOMS, ATOMS), 1)
    prefix = (row <= col).astype(F32)
    s0 = lax.broadcasted_iota(I32, (16, 16), 0)
    s1 = lax.broadcasted_iota(I32, (16, 16), 1)
    before = (((s0 >> 2) == (s1 >> 2)) & (s1 < s0)).astype(F32)
    rank = jnp.dot(hits, prefix, preferred_element_type=F32)
    earlier = jnp.dot(before, hits, preferred_element_type=F32)
    rank = rank + jnp.dot(earlier, jnp.ones((ATOMS, ATOMS), F32), preferred_element_type=F32)
    rank = jnp.where(hits > 0.5, rank, 0.0)
    wanted = (lax.broadcasted_iota(I32, (REV, ATOMS), 0) + 1).astype(F32)
    place = lax.broadcasted_iota(I32, (1, ATOMS), 1)
    place = jnp.where(place < NDEV, place, place + (previous - 1) * NDEV)
    picked = []
    for b in range(BLK):
        total = jnp.zeros((REV, ATOMS), F32)
        for o in range(BLK):
            code = (place * BLK + o + 1).astype(F32)
            total = total + jnp.where(rank[b * BLK + o : b * BLK + o + 1] == wanted, code, 0.0)
        picked.append(total)
    picked = jnp.concatenate(picked, axis=0)
    codes = lax.dot_general(jnp.ones((8, ATOMS), F32), picked, NT, precision=HIGH, preferred_element_type=F32)
    found[...] = (codes + 0.5).astype(I32)
    copy = pltpu.make_async_copy(found, found_s, sem)
    copy.start()
    here = d >> 2

    def note(b, n, place, block):
        lst1[b, n] = place * ROWS1 + block
        lst2[b, n] = place * ROWS2 + block

    for b in range(BLK):

        def listing(k, n, b=b):
            cell = pairs[b, k]
            partner = owners_s[jnp.maximum(cell, 0)]
            region = partner >> 8
            slot = jnp.where(region == r, 0, jnp.where(region == r + 1 - 2 * odd, 1, 2))
            dev = (partner >> 2) & (NDEV - 1)
            offset = ((dev >> 2) - here + HALF) & (NZ - 1)
            note(b, n, slot * NDEV + (dev & 3) * NZ + offset, partner & 3)
            return n + (cell >= 0).astype(I32)

        cnt[b] = lax.fori_loop(0, SLOTS, listing, jnp.int32(0), unroll=True)
    copy.wait()
    for b in range(BLK):

        def reverse(k, n, b=b):
            code = found_s[0, b * REV + k]
            note(b, n, jnp.maximum(code - 1, 0) >> 2, (code - 1) & 3)
            return n + (code > 0).astype(I32)

        cnt[b] = lax.fori_loop(0, REV, reverse, cnt[b], unroll=8)


GROUP = 64


def groups():
    return [pl.ds(g, GROUP) for g in range(0, ATOMS, GROUP)]


def diagonal(g):
    return lax.broadcasted_iota(I32, (GROUP, ATOMS), 1) == lax.broadcasted_iota(I32, (GROUP, ATOMS), 0) + g.start


def descreen_kernel(
    where, pairs, owners_s, owners, types, charges, fields, out, lst1, lst2, cnt, home, acc, listed, found, found_s, sem
):
    r, d = where()
    find_partners(r, d, pairs, owners_s, owners, fields, lst1, lst2, cnt, listed, found, found_s, sem)
    sums = []
    for b in range(BLK):
        own = own_place(d) * ROWS1 + b
        rho_row = table(types[b : b + 1, :], type_radii) - radius_offset
        rows = [fields[own], fields[own + 4], fields[own + 8], rho_row, 8.0 / rho_row]
        spread(jnp.concatenate(rows + [jnp.zeros((3, ATOMS), F32)], axis=0), home)

        def tile(start, first):
            x, y, z, kind = (fields[start + 4 * f] for f in range(4))
            s = table(kind, type_scales) * (table(kind, type_radii) - radius_offset)
            for g in groups():
                hx, hy, hz, ha, hi = (home[f, g, :] for f in range(5))
                dx = hx - x
                dy = hy - y
                dz = hz - z
                r2 = dx * dx + dy * dy + dz * dz
                if first:
                    mask = diagonal(g)
                    acc[g, :] = jnp.where(mask, 0.0, h_term(jnp.where(mask, 1.0, r2), ha, hi, s))
                else:
                    acc[g, :] += h_term(r2, ha, hi, s)

        tile(own, True)

        def step(n, carry, b=b):
            tile(lst1[b, n], False)
            return carry

        lax.fori_loop(0, cnt[b], step, 0)
        sums.append(row_sums(acc[...]))
    descreen = 0.125 * jnp.concatenate(sums, axis=0)
    rho0 = table(types[...], type_radii)
    rho = rho0 - radius_offset
    psi = descreen * rho
    shaped = born_alpha * psi - born_beta * psi * psi + born_gamma * psi * psi * psi
    out[0:4, :] = 1.0 / (1.0 / rho - jnp.tanh(shaped) / rho0)
    out[4:8, :] = charges[...]


def descreen_stage(where, pairs, owner_map, types, charges, fields):
    smem = pl.BlockSpec(memory_space=pltpu.SMEM)
    vmem = pl.BlockSpec(memory_space=pltpu.VMEM)
    return pl.pallas_call(
        functools.partial(descreen_kernel, where),
        out_shape=(
            jax.ShapeDtypeStruct((ROWS2, ATOMS), F32),
            jax.ShapeDtypeStruct((BLK, LIST), I32),
            jax.ShapeDtypeStruct((BLK, LIST), I32),
            jax.ShapeDtypeStruct((BLK,), I32),
        ),
        in_specs=[smem, smem, vmem, vmem, vmem, vmem],
        out_specs=(vmem, smem, smem, smem),
        scratch_shapes=[
            pltpu.VMEM((5, ATOMS, ATOMS), F32),
            pltpu.VMEM((ATOMS, ATOMS), F32),
            pltpu.VMEM((ATOMS, ATOMS), F32),
            pltpu.VMEM((8, ATOMS), I32),
            pltpu.SMEM((8, ATOMS), I32),
            pltpu.SemaphoreType.DMA,
        ],
        name="descreen",
    )(pairs, owner_map, owner_map.reshape(16, ATOMS), types, charges, fields.reshape(-1, 1, ATOMS))


def energy_kernel(where, lst1, lst2, cnt, fields, radii, energy, forces, grad, home, acc):
    r, d = where()
    for b in range(BLK):
        own = own_place(d) * ROWS1 + b
        own2 = own_place(d) * ROWS2 + b
        radius = radii[pl.ds(own2, 1), :]
        charge = radii[pl.ds(own2 + 4, 1), :]
        inverse = 1.0 / radius
        rows = [fields[own], fields[own + 4], fields[own + 8], solvent_tau * charge, radius]
        rows.append((-0.25 * math.log2(math.e)) * inverse)
        spread(jnp.concatenate(rows + [jnp.zeros((2, ATOMS), F32)], axis=0), home)

        def tile(start, start2, first):
            x, y, z = (fields[start + 4 * f] for f in range(3))
            radius_j = radii[pl.ds(start2, 1), :]
            charge_j = radii[pl.ds(start2 + 4, 1), :]
            inverse_j = 1.0 / radius_j
            for g in groups():
                hx, hy, hz, hq, hr, hd = (home[f, g, :] for f in range(6))
                dx = hx - x
                dy = hy - y
                dz = hz - z
                r2 = dx * dx + dy * dy + dz * dz
                if first:
                    mask = diagonal(g)
                    r2 = jnp.where(mask, 1.0, r2)
                arg = r2 * (hd * inverse_j)
                damped = jnp.exp2(arg)
                inv = lax.rsqrt(r2 + hr * radius_j * damped)
                e = hq * charge_j * inv
                if first:
                    e = jnp.where(mask, 0.0, e)
                e3 = e * (inv * inv)
                e3d = e3 * damped
                pull = e3 - 0.25 * e3d
                terms = (pull * dx, pull * dy, pull * dz, e, (e3d * radius_j) * (1.0 - math.log(2.0) * arg))
                for f in range(5):
                    if first:
                        acc[f, g, :] = terms[f]
                    else:
                        acc[f, g, :] += terms[f]

        tile(own, own2, True)

        def step(n, carry, b=b):
            tile(lst1[b, n], lst2[b, n], False)
            return carry

        lax.fori_loop(0, cnt[b], step, 0)
        for f in range(3):
            forces[f, b : b + 1, :] = -row_sums(acc[f])
        self_e = solvent_tau * charge * charge
        energy[b : b + 1, :] = -0.5 * row_sums(acc[3]) - 0.5 * self_e * inverse
        grad[b : b + 1, :] = 0.5 * row_sums(acc[4]) + 0.5 * self_e * inverse * inverse


def energy_stage(where, lst1, lst2, cnt, fields, radii):
    smem = pl.BlockSpec(memory_space=pltpu.SMEM)
    vmem = pl.BlockSpec(memory_space=pltpu.VMEM)
    return pl.pallas_call(
        functools.partial(energy_kernel, where),
        out_shape=(
            jax.ShapeDtypeStruct((BLK, ATOMS), F32),
            jax.ShapeDtypeStruct((3, BLK, ATOMS), F32),
            jax.ShapeDtypeStruct((BLK, ATOMS), F32),
        ),
        in_specs=[smem, smem, smem, vmem, vmem],
        out_specs=(vmem, vmem, vmem),
        scratch_shapes=[pltpu.VMEM((6, ATOMS, ATOMS), F32), pltpu.VMEM((5, ATOMS, ATOMS), F32)],
        name="energy",
    )(lst1, lst2, cnt, fields.reshape(-1, 1, ATOMS), radii.reshape(-1, ATOMS))


def shards(positions, charges, types, pairs, owner_map):
    fields = gather_fields(positions, types, pairs)
    mine, lst1, lst2, cnt = descreen_stage(ids_here, pairs, owner_map, types, charges, fields)
    radii = gather_radii(mine)
    energy, forces, grad = energy_stage(ids_here, lst1, lst2, cnt, fields, radii)
    return (mine[:BLK], energy, forces, grad)


def solution(mesh):
    placed = (
        P(None, ("region", "dev"), None),
        P(("region", "dev"), None),
        P(("region", "dev"), None),
        P(("region", "dev"), None),
        P(),
    )
    return jax.shard_map(
        shards,
        mesh=mesh,
        in_specs=placed,
        out_specs=(
            P(("region", "dev"), None),
            P(("region", "dev"), None),
            P(None, ("region", "dev"), None),
            P(("region", "dev"), None),
        ),
        check_vma=False,
    )
```

time: 134 us -> 88.4 us (0.66)
  the two profiles are of different devices: /device:TPU:13 before, /device:TPU:1 now
where the time goes in v2:
time: 88.4 us; the launch traced here: 88.6 us
  Pallas kernels  86.7 us (98%)
  local copies, waits for them, and re-layouts  1.27 us (1%)
    pallas_call x1, Pallas kernels, gather_fields(): pl.pallas_call(fields_kernel, out_shape=jax.ShapeDtypeStruct((3, NY, NZ,...  36.2 us
    pallas_call x1, Pallas kernels, gather_radii(): pl.pallas_call(radii_kernel, out_shape=jax.ShapeDtypeStruct((3, NY, NZ, R...  19.4 us
    pallas_call x1, Pallas kernels, descreen_stage(): pl.pallas_call(functools.partial(descreen_kernel, where), out_shape=(jax....  17 us
    pallas_call x1, Pallas kernels, energy_stage(): pl.pallas_call(functools.partial(energy_kernel, where), out_shape=(jax.Sh...  14.2 us

profile of v2, /device:TPU:1, one launch (start us, length us, event | category | flops | bytes accessed | tf_op | source)
XLA Modules:
  0.0 88.6 jit_solution(1340852672495904999)
XLA Ops:
  0.6 36.2 %gather_fields.1 = f32[3,4,16,17,1,128]{5,4,3,2,1,0:T(1,128)} custom-call(s32[4,13]{1,0:T(4,128)} %pairs.3, f32[3,4,128]{2,1,0:T(4,128)} %pos.1, s32[4,128]{1,0:T(4,128)} %types.3), custom_call_target="tpu_custom_call" | custom-call | tf_op jit(solution)/shard_map/gather_fields/pallas_call | solution.py:161
  36.8 17.0 %descreen.1 = (f32[8,128]{1,0:T(8,128)}, s32[4,64]{1,0:T(4,128)}, s32[4,64]{1,0:T(4,128)}, s32[4]{0:T(128)}) custom-call(s32[4,13]{1,0:T(4,128)} %pairs.3, s32[2048]{0:T(1024)} %owners_s.1, s32[16,128]{1,0:T(8,128)} %bitcast.6, s32[4,128]{1,0:T(4,128)} %types.3, f32[4,128]{1,0:T(4,128)} %charges.1, f32[3264,1,128]{2,1,0:T(1,128)} %bitcast.3), custom_call_target="tpu_custom_call" | custom-call | tf_op jit(solution)/shard_map/descreen/pallas_call | solution.py:356
  53.8 1.3 %slice.3 = f32[4,128]{1,0:T(4,128)} slice(f32[8,128]{1,0:T(8,128)} %get-tuple-element.11.x), slice={[0:4], [0:128]} | slice | bytes 4096 | tf_op jit(solution)/shard_map/slice | solution.py:456
  55.1 19.4 %gather_radii.1 = f32[3,4,16,8,128]{4,3,2,1,0:T(8,128)} custom-call(f32[8,128]{1,0:T(8,128)} %get-tuple-element.11.x), custom_call_target="tpu_custom_call" | custom-call | tf_op jit(solution)/shard_map/gather_radii/pallas_call | solution.py:178
  74.4 14.2 %energy.1 = (f32[4,128]{1,0:T(4,128)}, f32[3,4,128]{2,1,0:T(4,128)}, f32[4,128]{1,0:T(4,128)}) custom-call(s32[4,64]{1,0:T(4,128)} %get-tuple-element.12.lst1, s32[4,64]{1,0:T(4,128)} %get-tuple-element.13.lst2, s32[4]{0:T(128)} %get-tuple-element.14.cnt, f32[3264,1,128]{2,1,0:T(1,128)} %bitcast.4, f32[1536,128]{1,0:T(8,128)} %bitcast.5), custom_call_target="tpu_custom_call" | custom-call | tf_op jit(solution)/shard_map/energy/pallas_call | solution.py:437

commit v3 on v2

v3 whole, which is shorter than its diff:
```python
import functools
import math

import jax
import jax.numpy as jnp
import numpy as np
from jax import lax
from jax.experimental import pallas as pl
from jax.experimental.pallas import tpu as pltpu
from jax.sharding import PartitionSpec as P

type_radii = (1.2, 1.7, 1.55, 1.52, 1.85, 1.8)
type_scales = (0.85, 0.72, 0.79, 0.85, 0.86, 0.96)
radius_offset = 0.09
born_alpha = 1.0
born_beta = 0.8
born_gamma = 4.85
solvent_tau = 1.0 - 1.0 / 78.5

MESH = pl.DeviceIdType.MESH
NREG = 8
NZ = 16
NY = 4
NDEV = NZ * NY
BLK = 4
SLOTS = 13
ATOMS = 128
ROWS1 = 17
ROWS2 = 8
REGION_BLOCKS = NDEV * BLK
REV = 32
LIST = 64
HALF = NZ // 2
REACH = 4
PIECES = ((4, 13), (0, 4), (13, 16))
F32 = jnp.float32
I32 = jnp.int32
HIGH = lax.Precision.HIGHEST
NT = (((1,), (1,)), ((), ()))


scaled_values = [float(np.float32(s) * (np.float32(v) - np.float32(radius_offset))) for s, v in zip(type_scales, type_radii)]


def table(types, values):
    out = jnp.full(types.shape, values[0], F32)
    for i in range(1, len(values)):
        out = jnp.where(types == i, F32(values[i]), out)
    return out


TILES = 2 * SLOTS
NOWHERE = -1e30


def far_peers():
    r = lax.axis_index("region")
    d = lax.axis_index("dev")
    z = d // NY
    y = d % NY
    odd = r % 2
    hops = sorted((k for k in range(-REACH, REACH + 1) if k), key=abs)
    along = {k: (r, (z + k + NZ) % NZ * NY + y) for k in hops}
    across = [(r, z * NY + (y + k) % NY) for k in range(1, NY)]
    sibling = (r + 1 - 2 * odd, d)
    beside = ((r + 2 * odd - 1 + NREG) % NREG, d)
    return r, d, y, along, across, sibling, beside


def gather_body(peers, out, zsend, zrecv, ysend, yrecv, fsend, frecv, idle):
    r, d, y, along, across, sibling, beside = peers
    sends = []

    def send(src, dst, ssem, rsem, to):
        copy = pltpu.make_async_remote_copy(
            src_ref=src, dst_ref=dst, send_sem=ssem, recv_sem=rsem, device_id=to, device_id_type=MESH
        )
        copy.start()
        sends.append(copy)

    def wait_for(dst, rsem):
        pltpu.make_async_remote_copy(
            src_ref=dst, dst_ref=dst, send_sem=rsem, recv_sem=rsem, device_id=sibling, device_id_type=MESH
        ).wait_recv()

    def part(slot, yy, a, b):
        return out.at[pl.ds((slot * NY + yy) * NZ + a, b - a)]

    def single(o):
        return part(0, y, o, o + 1)

    for n, k in enumerate(along):
        send(single(HALF), single(HALF - k), zsend.at[n], zrecv.at[HALF - k], along[k])
    idle()

    def forward(yy, k, p):
        span = PIECES[p]
        send(part(0, yy, *span), part(2, yy, *span), fsend.at[1, k, p], frecv.at[1, k, p], beside)
        send(part(0, yy, *span), part(1, yy, *span), fsend.at[0, k, p], frecv.at[0, k, p], sibling)

    low, high = HALF - REACH, HALF + REACH + 1
    for p, span in enumerate(PIECES):
        if p == 0:
            for k in along:
                wait_for(single(HALF + k), zrecv.at[HALF + k])
            send(part(0, y, low, HALF), part(0, y, 0, low), zsend.at[2 * REACH], zrecv.at[0], along[REACH])
            send(
                part(0, y, HALF + 1, HALF + REACH),
                part(0, y, high, NZ),
                zsend.at[2 * REACH + 1],
                zrecv.at[high],
                along[-REACH],
            )
        else:
            wait_for(part(0, y, *span), zrecv.at[span[0]])
        for k in (2, 1, 3):
            send(part(0, y, *span), part(0, y, *span), ysend.at[k - 1, p], yrecv.at[k - 1, p], across[k - 1])
        forward(y, 0, p)
        for q in [p - 1] * (p > 0) + [p] * (p == len(PIECES) - 1):
            for k in (1, 3, 2):
                yy = (y + NY - k) % NY
                wait_for(part(0, yy, *PIECES[q]), yrecv.at[k - 1, q])
                forward(yy, k, q)
    for p, span in enumerate(PIECES):
        for k in range(NY):
            yy = (y + NY - k) % NY
            wait_for(part(1, yy, *span), frecv.at[0, k, p])
            wait_for(part(2, yy, *span), frecv.at[1, k, p])
    for copy in sends:
        copy.wait_send()


def gather_scratch():
    dma = pltpu.SemaphoreType.DMA
    parts = len(PIECES)
    return [
        dma((NZ,)),
        dma((NZ,)),
        dma((NY - 1, parts)),
        dma((NY - 1, parts)),
        dma((2, NY, parts)),
        dma((2, NY, parts)),
    ]


GATHER_SEMS = len(gather_scratch())


def spread(rows, refs):
    rows = list(rows) + [jnp.zeros((1, ATOMS), F32)] * (8 - len(rows))
    turned = jnp.transpose(jnp.concatenate(rows, axis=0))
    for f, ref in enumerate(refs):
        ref[...] = jnp.broadcast_to(turned[:, f : f + 1], (ATOMS, ATOMS))


def row_sums(values):
    ones = jnp.ones((8, ATOMS), jnp.bfloat16)
    total = jnp.zeros((8, ATOMS), F32)
    for step in range(3):
        part = values.astype(jnp.bfloat16)
        values = values - part.astype(F32)
        total = total + lax.dot_general(ones, part, NT, preferred_element_type=F32)
    return total[0:1]


def h_term(r2, a, ia8, s):
    ir = lax.rsqrt(r2)
    r = r2 * ir
    upper = r + s
    gap = s - r
    lower = jnp.maximum(a, jnp.abs(gap))
    il = 1.0 / lower
    iu = 1.0 / upper
    value = (il - iu) * (4.0 + (il + iu) * (s * s * ir - r)) + (ir + ir) * jnp.log(lower * iu)
    value = value + jnp.where(a < gap, ia8 - 8.0 * il, 0.0)
    return jnp.where(upper > a, value, 0.0)


def listed_codes(r, d, pairs, owners):
    odd = r % 2
    here = d // NY
    lane = lax.broadcasted_iota(I32, (1, ATOMS), 1)
    row = jnp.zeros((1, ATOMS), I32)
    for b in range(BLK):
        for k in range(SLOTS):
            cell = pairs[b, k]
            partner = owners[jnp.clip(cell, 0, NREG * REGION_BLOCKS - 1)]
            region = partner >> 8
            slot = jnp.where(region == r, 0, jnp.where(region == r + 1 - 2 * odd, 1, 2))
            offset = (((partner >> 4) & (NZ - 1)) - here + HALF) & (NZ - 1)
            place = slot * NDEV + ((partner >> 2) & (NY - 1)) * NZ + offset
            code = jnp.where(cell >= 0, place * BLK + (partner & (BLK - 1)) + 1, 0)
            row = jnp.where(lane == b * SLOTS + k, code, row)
    return row.astype(F32)


def merge_partners(r, forward, cells, known, found):
    previous = 2 - r % 2
    sub = lax.broadcasted_iota(I32, (16, ATOMS), 0)
    lane = lax.broadcasted_iota(I32, (16, ATOMS), 1)
    hits = jnp.zeros((16, ATOMS), F32)
    first = (sub & 3) * SLOTS
    for b in range(BLK):
        match = (known == cells[b]).astype(F32)
        pick = (((sub >> 2) == b) & (lane >= first) & (lane < first + SLOTS)).astype(F32)
        hits = hits + lax.dot_general(pick, match, NT, preferred_element_type=F32)
    start = (sub >> 2) * SLOTS
    listed = jnp.where((forward > 0.5) & (lane >= start) & (lane < start + SLOTS), 1.0, 0.0)
    row = lax.broadcasted_iota(I32, (ATOMS, ATOMS), 0)
    col = lax.broadcasted_iota(I32, (ATOMS, ATOMS), 1)
    prefix = (row <= col).astype(F32)
    ones = jnp.ones((ATOMS, ATOMS), F32)
    s0 = lax.broadcasted_iota(I32, (16, 16), 0)
    s1 = lax.broadcasted_iota(I32, (16, 16), 1)
    before = (((s0 >> 2) == (s1 >> 2)) & (s1 < s0)).astype(F32)
    earlier = jnp.dot(before, hits, preferred_element_type=F32) + listed
    rank = jnp.dot(hits, prefix, preferred_element_type=F32) + jnp.dot(earlier, ones, preferred_element_type=F32)
    rank = jnp.where(hits > 0.5, rank, 0.0)
    order = jnp.where(listed > 0.5, jnp.dot(listed, prefix, preferred_element_type=F32), 0.0)
    wanted = (lax.broadcasted_iota(I32, (REV, ATOMS), 0) + 1).astype(F32)
    place = lax.broadcasted_iota(I32, (1, ATOMS), 1)
    place = jnp.where(place < NDEV, place, place + (previous - 1) * NDEV)
    picked = []
    for b in range(BLK):
        total = jnp.where(order[b * BLK : b * BLK + 1] == wanted, forward, 0.0)
        for o in range(BLK):
            code = (place * BLK + o + 1).astype(F32)
            total = total + jnp.where(rank[b * BLK + o : b * BLK + o + 1] == wanted, code, 0.0)
        picked.append(total)
    picked = jnp.concatenate(picked, axis=0)
    codes = lax.dot_general(jnp.ones((8, ATOMS), F32), picked, NT, precision=HIGH, preferred_element_type=F32)
    found[...] = (codes + 0.5).astype(I32)


GROUP = 64


GROUP1 = 64
GROUP2 = 16
WIDE = 2


def groups(size=GROUP):
    return [pl.ds(g, size) for g in range(0, ATOMS, size)]


def diagonal(g):
    return lax.broadcasted_iota(I32, (GROUP, ATOMS), 1) == lax.broadcasted_iota(I32, (GROUP, ATOMS), 0) + g.start


def whole_kernel(
    pairs, owners_s, owners, pos, charges, types, out,
    x1, x2, fields, radii, home1, home2, acc1, acc2, geo, listed, found, found_s, local, *sems
):
    peers = far_peers()
    r, d, y, along, across, sibling, beside = peers
    everyone = list(along.values()) + across + [sibling, beside]
    barrier = pltpu.get_barrier_semaphore()
    for peer in everyone:
        pl.semaphore_signal(barrier, inc=1, device_id=peer, device_id_type=MESH)

    for b in range(BLK):
        for f in range(3):
            x1[0, 4 * f + b, :, :] = pos[f, b : b + 1, :]
        x1[0, 12 + b, :, :] = types[b : b + 1, :].astype(F32)
    lane = lax.broadcasted_iota(I32, (1, ATOMS), 1)
    row = jnp.full((1, ATOMS), -1, I32)
    for b in range(BLK):
        for k in range(SLOTS):
            row = jnp.where(lane == b * SLOTS + k, pairs[b, k], row)
    x1[0, 16, :, :] = row.astype(F32)
    ids = lax.broadcasted_iota(I32, (16, ATOMS), 0) * ATOMS + lax.broadcasted_iota(I32, (16, ATOMS), 1)
    held = owners[...]
    base = r * REGION_BLOCKS + d * BLK
    cells = [jnp.sum(jnp.where(held == base + b, ids, 0).astype(F32)) for b in range(BLK)]
    forward = listed_codes(r, d, pairs, owners_s)

    own_place = pl.ds(y * NZ + HALF, 1)

    def load_own(src, dst):
        copy = pltpu.make_async_copy(src, dst.at[own_place], local)
        copy.start()
        copy.wait()

    rho0 = table(types[...], type_radii)
    rho = rho0 - radius_offset
    scaled = table(types[...], type_scales) * rho

    def own_rows(b):
        return [pos[f, b : b + 1, :] for f in range(3)]

    def geometry(home, rows):
        dx, dy, dz = (h - v for h, v in zip(home, rows))
        return dx, dy, dz, dx * dx + dy * dy + dz * dz

    def own_descreen():
        for b in range(BLK):
            rho_b = rho[b : b + 1]
            spread(own_rows(b) + [rho_b, 8.0 / rho_b], [home1.at[b, f] for f in range(5)])
        for b in range(BLK):
            for g in groups():
                hx, hy, hz, ha, hi = (home1[b, f, g, :] for f in range(5))
                r2 = geometry((hx, hy, hz), own_rows(b))[3]
                mask = diagonal(g)
                acc1[b, g, :] = jnp.where(mask, 0.0, h_term(jnp.where(mask, 1.0, r2), ha, hi, scaled[b : b + 1]))

    load_own(x1, fields)
    pl.semaphore_wait(barrier, len(everyone))
    gather_body(peers, fields, *sems[:GATHER_SEMS], own_descreen)

    previous = 2 - r % 2
    for half, start in enumerate((0, previous * NDEV)):

        def take(n, carry, half=half, start=start):
            listed[pl.ds(half * NDEV + n, 1), :] = fields[start + n, 16]
            return carry

        lax.fori_loop(0, NDEV, take, 0, unroll=16)
    merge_partners(r, forward, cells, listed[...], found)
    copy = pltpu.make_async_copy(found, found_s, local)
    copy.start()
    copy.wait()

    def partner(b, n):
        code = found_s[0, b * REV + n]
        where = jnp.clip(code, 1, 3 * REGION_BLOCKS) - 1
        return code > 0, where >> 2, where & (BLK - 1)

    for b in range(BLK):

        def descreen_step(m, carry, b=b):
            sides = []
            for i in range(WIDE):
                live, place, block = partner(b, WIDE * m + i)
                rows = [fields[place, 4 * f + block] for f in range(3)]
                kind = fields[place, 12 + block]
                s = table(kind, scaled_values)
                sides.append((rows, jnp.where(live, s, NOWHERE)))
            for g in groups(GROUP1):
                hx, hy, hz, ha, hi = (home1[b, f, g, :] for f in range(5))
                terms = [h_term(geometry((hx, hy, hz), rows)[3], ha, hi, s) for rows, s in sides]
                acc1[b, g, :] += functools.reduce(jnp.add, terms)
            return carry

        lax.fori_loop(0, TILES // WIDE, descreen_step, 0)

    descreen = 0.125 * jnp.concatenate([row_sums(acc1[b]) for b in range(BLK)], axis=0)
    psi = descreen * rho
    shaped = born_alpha * psi - born_beta * psi * psi + born_gamma * psi * psi * psi
    born = 1.0 / (1.0 / rho - jnp.tanh(shaped) / rho0)
    out[0:4, :] = born
    for b in range(BLK):
        x2[0, b, :, :] = born[b : b + 1]
        x2[0, 4 + b, :, :] = charges[b : b + 1, :]
    load_own(x2, radii)

    inverse = 1.0 / born

    def energy_terms(geom, home, radius_j, inverse_j, charge_j, mask=None):
        dx, dy, dz, r2 = geom
        hq, hr, hd = home
        arg = r2 * (hd * inverse_j)
        damped = jnp.exp2(arg)
        inv = lax.rsqrt(r2 + hr * radius_j * damped)
        e = hq * charge_j * inv
        if mask is not None:
            e = jnp.where(mask, 0.0, e)
        e3 = e * (inv * inv)
        e3d = e3 * damped
        pull = e3 - 0.25 * e3d
        return pull * dx, pull * dy, pull * dz, e, (e3d * radius_j) * (1.0 - math.log(2.0) * arg)

    def while_radii_travel():
        for b in range(BLK):

            def geometry_step(n, carry, b=b):
                live, place, block = partner(b, n)
                rows = [fields[place, 4 * f + block] for f in range(3)]
                for g in groups():
                    geom = geometry([home1[b, f, g, :] for f in range(3)], rows)
                    for f in range(4):
                        geo[b * TILES + n, f, g, :] = geom[f]
                return carry

            lax.fori_loop(0, TILES, geometry_step, 0)
        for b in range(BLK):
            one = slice(b, b + 1)
            scale = (-0.25 * math.log2(math.e)) * inverse[one]
            spread([solvent_tau * charges[one, :], born[one], scale], [home2.at[b, f] for f in range(3)])
        for b in range(BLK):
            one = slice(b, b + 1)
            for g in groups():
                dx, dy, dz, r2 = geometry([home1[b, f, g, :] for f in range(3)], own_rows(b))
                mask = diagonal(g)
                geom = (dx, dy, dz, jnp.where(mask, 1.0, r2))
                home = [home2[b, f, g, :] for f in range(3)]
                terms = energy_terms(geom, home, born[one], inverse[one], charges[one, :], mask)
                for f in range(5):
                    acc2[b, f, g, :] = terms[f]

    gather_body(peers, radii, *sems[GATHER_SEMS:], while_radii_travel)

    for b in range(BLK):

        def energy_step(m, carry, b=b):
            sides = []
            for i in range(WIDE):
                live, place, block = partner(b, WIDE * m + i)
                radius_j = radii[place, block]
                charge_j = jnp.where(live, radii[place, 4 + block], 0.0)
                sides.append((b * TILES + WIDE * m + i, radius_j, 1.0 / radius_j, charge_j))
            for g in groups(GROUP2):
                home = [home2[b, f, g, :] for f in range(3)]
                terms = [energy_terms([geo[t, f, g, :] for f in range(4)], home, *rest) for t, *rest in sides]
                for f in range(5):
                    acc2[b, f, g, :] += functools.reduce(jnp.add, [term[f] for term in terms])
            return carry

        lax.fori_loop(0, TILES // WIDE, energy_step, 0)

    for b in range(BLK):
        one = slice(b, b + 1)
        for f in range(3):
            out[8 + 4 * f + b : 9 + 4 * f + b, :] = -row_sums(acc2[b, f])
        self_e = solvent_tau * charges[one, :] * charges[one, :]
        out[4 + b : 5 + b, :] = -0.5 * row_sums(acc2[b, 3]) - 0.5 * self_e * inverse[one]
        out[20 + b : 21 + b, :] = 0.5 * row_sums(acc2[b, 4]) + 0.5 * self_e * inverse[one] * inverse[one]


def whole(positions, charges, types, pairs, owner_map):
    smem = pl.BlockSpec(memory_space=pltpu.SMEM)
    vmem = pl.BlockSpec(memory_space=pltpu.VMEM)
    square = (ATOMS, ATOMS)
    return pl.pallas_call(
        whole_kernel,
        out_shape=jax.ShapeDtypeStruct((24, ATOMS), F32),
        in_specs=[smem, smem, vmem, vmem, vmem, vmem],
        out_specs=vmem,
        scratch_shapes=[
            pltpu.VMEM((1, ROWS1, 1, ATOMS), F32),
            pltpu.VMEM((1, ROWS2, 1, ATOMS), F32),
            pltpu.VMEM((3 * NDEV, ROWS1, 1, ATOMS), F32),
            pltpu.VMEM((3 * NDEV, ROWS2, 1, ATOMS), F32),
            pltpu.VMEM((BLK, 5) + square, F32),
            pltpu.VMEM((BLK, 3) + square, F32),
            pltpu.VMEM((BLK,) + square, F32),
            pltpu.VMEM((BLK, 5) + square, F32),
            pltpu.VMEM((BLK * TILES, 4) + square, F32),
            pltpu.VMEM(square, F32),
            pltpu.VMEM((8, ATOMS), I32),
            pltpu.SMEM((8, ATOMS), I32),
            pltpu.SemaphoreType.DMA,
        ]
        + gather_scratch()
        + gather_scratch(),
        compiler_params=pltpu.CompilerParams(
            collective_id=0, has_side_effects=True, vmem_limit_bytes=56 * 1024 * 1024
        ),
        name="whole",
    )(pairs, owner_map, owner_map.reshape(16, ATOMS), positions, charges, types)


def unpack_kernel(packed, born, energy, forces, grad):
    born[...] = packed[0:4, :]
    energy[...] = packed[4:8, :]
    for f in range(3):
        forces[f] = packed[8 + 4 * f : 12 + 4 * f, :]
    grad[...] = packed[20:24, :]


def shards(positions, charges, types, pairs, owner_map):
    packed = whole(positions, charges, types, pairs, owner_map)
    flat = jax.ShapeDtypeStruct((BLK, ATOMS), F32)
    vmem = pl.BlockSpec(memory_space=pltpu.VMEM)
    return pl.pallas_call(
        unpack_kernel,
        out_shape=(flat, flat, jax.ShapeDtypeStruct((3, BLK, ATOMS), F32), flat),
        in_specs=[vmem],
        out_specs=(vmem,) * 4,
        name="unpack",
    )(packed)


def solution(mesh):
    placed = (
        P(None, ("region", "dev"), None),
        P(("region", "dev"), None),
        P(("region", "dev"), None),
        P(("region", "dev"), None),
        P(),
    )
    return jax.shard_map(
        shards,
        mesh=mesh,
        in_specs=placed,
        out_specs=(
            P(("region", "dev"), None),
            P(("region", "dev"), None),
            P(None, ("region", "dev"), None),
            P(("region", "dev"), None),
        ),
        check_vma=False,
    )
```

time: 88.4 us -> 72.6 us (0.82)
  Pallas kernels: 86.7 us -> 71.8 us
  local copies, waits for them, and re-layouts: 1.27 us -> 0 us
    pallas_call x4 -> x2, Pallas kernels: 86.7 us -> 71.8 us  [the longest x1 70.5 us: whole(): pl.pallas_call(whole_kernel, out_shape=jax.ShapeDtypeStruct((24, ATOMS),...]
    slice x1 -> x0, local copies, waits for them, and re-layouts: 1.27 us -> none  [shards(): return (mine[:BLK], energy, forces, grad)]
where the time goes in v3:
time: 72.6 us; the launch traced here: 72.4 us
  Pallas kernels  71.8 us (99%)
    pallas_call x1, Pallas kernels, whole(): pl.pallas_call(whole_kernel, out_shape=jax.ShapeDtypeStruct((24, ATOMS),...  70.5 us

profile of v3, /device:TPU:1, one launch (start us, length us, event | category | flops | bytes accessed | tf_op | source)
XLA Modules:
  0.0 72.4 jit_solution(1405807452738559747)
XLA Ops:
  0.6 70.5 %whole.1.packed = f32[24,128]{1,0:T(8,128)} custom-call(s32[4,13]{1,0:T(4,128)} %pairs.1, s32[2048]{0:T(1024)} %owners_s.1, s32[16,128]{1,0:T(8,128)} %bitcast.1, f32[3,4,128]{2,1,0:T(4,128)} %pos.1, f32[4,128]{1,0:T(4,128)} %charges.1, s32[4,128]{1,0:T(4,128)} %types.1), custom_call_target="tpu_custom_call" | custom-call | tf_op jit(solution)/shard_map/whole/pallas_call | solution.py:434
  71.1 1.3 %unpack.1 = (f32[4,128]{1,0:T(4,128)}, f32[4,128]{1,0:T(4,128)}, f32[3,4,128]{2,1,0:T(4,128)}, f32[4,128]{1,0:T(4,128)}) custom-call(f32[24,128]{1,0:T(8,128)} %whole.1.packed), custom_call_target="tpu_custom_call" | custom-call | tf_op jit(solution)/shard_map/unpack/pallas_call | solution.py:475

commit v4 on v3

--- a/solution.py
+++ b/solution.py
@@ -33,9 +33,11 @@
 HALF = NZ // 2
 REACH = 4
 PIECES = ((4, 13), (0, 4), (13, 16))
+ORDER = ((0,), (0, (1, 3)), (1,), (2,), (0, (2,)), (1, (1, 3, 2)), (2, (1, 3, 2)))
+DIRECT1 = (False, True, True)
+DIRECT2 = (False, True, True)
 F32 = jnp.float32
 I32 = jnp.int32
-HIGH = lax.Precision.HIGHEST
 NT = (((1,), (1,)), ((), ()))
 
 
@@ -63,11 +65,12 @@
     along = {k: (r, (z + k + NZ) % NZ * NY + y) for k in hops}
     across = [(r, z * NY + (y + k) % NY) for k in range(1, NY)]
     sibling = (r + 1 - 2 * odd, d)
-    beside = ((r + 2 * odd - 1 + NREG) % NREG, d)
+    other = (r + 2 * odd - 1 + NREG) % NREG
+    beside = [(other, z * NY + (y + k) % NY) for k in range(NY)]
     return r, d, y, along, across, sibling, beside
 
 
-def gather_body(peers, out, zsend, zrecv, ysend, yrecv, fsend, frecv, idle):
+def gather_body(peers, direct, out, zsend, zrecv, ysend, yrecv, fsend, frecv, idle):
     r, d, y, along, across, sibling, beside = peers
     sends = []
 
@@ -95,11 +98,14 @@
 
     def forward(yy, k, p):
         span = PIECES[p]
-        send(part(0, yy, *span), part(2, yy, *span), fsend.at[1, k, p], frecv.at[1, k, p], beside)
+        if not direct[p]:
+            send(part(0, yy, *span), part(2, yy, *span), fsend.at[1, k, p], frecv.at[1, k, p], beside[0])
         send(part(0, yy, *span), part(1, yy, *span), fsend.at[0, k, p], frecv.at[0, k, p], sibling)
 
     low, high = HALF - REACH, HALF + REACH + 1
-    for p, span in enumerate(PIECES):
+
+    def along_done(p):
+        span = PIECES[p]
         if p == 0:
             for k in along:
                 wait_for(single(HALF + k), zrecv.at[HALF + k])
@@ -115,12 +121,21 @@
             wait_for(part(0, y, *span), zrecv.at[span[0]])
         for k in (2, 1, 3):
             send(part(0, y, *span), part(0, y, *span), ysend.at[k - 1, p], yrecv.at[k - 1, p], across[k - 1])
+        for k in (2, 1, 3, 0) if direct[p] else ():
+            send(part(0, y, *span), part(2, y, *span), fsend.at[1, k, p], frecv.at[1, k, p], beside[k])
         forward(y, 0, p)
-        for q in [p - 1] * (p > 0) + [p] * (p == len(PIECES) - 1):
-            for k in (1, 3, 2):
-                yy = (y + NY - k) % NY
-                wait_for(part(0, yy, *PIECES[q]), yrecv.at[k - 1, q])
-                forward(yy, k, q)
+
+    def across_done(p, ks):
+        for k in ks:
+            yy = (y + NY - k) % NY
+            wait_for(part(0, yy, *PIECES[p]), yrecv.at[k - 1, p])
+            forward(yy, k, p)
+
+    for leg in ORDER:
+        if len(leg) == 1:
+            along_done(*leg)
+        else:
+            across_done(*leg)
     for p, span in enumerate(PIECES):
         for k in range(NY):
             yy = (y + NY - k) % NY
@@ -154,13 +169,8 @@
 
 
 def row_sums(values):
-    ones = jnp.ones((8, ATOMS), jnp.bfloat16)
-    total = jnp.zeros((8, ATOMS), F32)
-    for step in range(3):
-        part = values.astype(jnp.bfloat16)
-        values = values - part.astype(F32)
-        total = total + lax.dot_general(ones, part, NT, preferred_element_type=F32)
-    return total[0:1]
+    eye = lax.broadcasted_iota(I32, values.shape, 0) == lax.broadcasted_iota(I32, values.shape, 1)
+    return jnp.sum(jnp.where(eye, jnp.sum(values, axis=1, keepdims=True), 0.0), axis=0, keepdims=True)
 
 
 def h_term(r2, a, ia8, s):
@@ -171,7 +181,7 @@
     lower = jnp.maximum(a, jnp.abs(gap))
     il = 1.0 / lower
     iu = 1.0 / upper
-    value = (il - iu) * (4.0 + (il + iu) * (s * s * ir - r)) + (ir + ir) * jnp.log(lower * iu)
+    value = (il - iu) * (4.0 + (il + iu) * (s * s * ir - r)) + ((2.0 * math.log(2.0)) * ir) * lax.log2(lower * iu)
     value = value + jnp.where(a < gap, ia8 - 8.0 * il, 0.0)
     return jnp.where(upper > a, value, 0.0)
 
@@ -228,8 +238,7 @@
             total = total + jnp.where(rank[b * BLK + o : b * BLK + o + 1] == wanted, code, 0.0)
         picked.append(total)
     picked = jnp.concatenate(picked, axis=0)
-    codes = lax.dot_general(jnp.ones((8, ATOMS), F32), picked, NT, precision=HIGH, preferred_element_type=F32)
-    found[...] = (codes + 0.5).astype(I32)
+    found[...] = jnp.broadcast_to((row_sums(picked) + 0.5).astype(I32), found.shape)
 
 
 GROUP = 64
@@ -249,15 +258,23 @@
 
 
 def whole_kernel(
-    pairs, owners_s, owners, pos, charges, types, out,
-    x1, x2, fields, radii, home1, home2, acc1, acc2, geo, listed, found, found_s, local, *sems
+    pairs_in, owners_s_in, owners_in, pos_in, charges_in, types_in, out,
+    pairs, owners_s, owners, pos, charges, types, brought, x1, x2, fields, radii, home1, home2, acc1, acc2, geo, listed, found, found_s, local, *sems
 ):
+    targets = (pairs, owners_s, owners, pos, charges, types)
+    sources = (pairs_in, owners_s_in, owners_in, pos_in, charges_in, types_in)
+    inputs = [pltpu.make_async_copy(src, dst, brought.at[i]) for i, (src, dst) in enumerate(zip(sources, targets))]
+    for copy in inputs:
+        copy.start()
     peers = far_peers()
     r, d, y, along, across, sibling, beside = peers
-    everyone = list(along.values()) + across + [sibling, beside]
+    everyone = list(along.values()) + across + [sibling] + beside
     barrier = pltpu.get_barrier_semaphore()
     for peer in everyone:
         pl.semaphore_signal(barrier, inc=1, device_id=peer, device_id_type=MESH)
+
+    for copy in inputs:
+        copy.wait()
 
     for b in range(BLK):
         for f in range(3):
@@ -269,12 +286,6 @@
         for k in range(SLOTS):
             row = jnp.where(lane == b * SLOTS + k, pairs[b, k], row)
     x1[0, 16, :, :] = row.astype(F32)
-    ids = lax.broadcasted_iota(I32, (16, ATOMS), 0) * ATOMS + lax.broadcasted_iota(I32, (16, ATOMS), 1)
-    held = owners[...]
-    base = r * REGION_BLOCKS + d * BLK
-    cells = [jnp.sum(jnp.where(held == base + b, ids, 0).astype(F32)) for b in range(BLK)]
-    forward = listed_codes(r, d, pairs, owners_s)
-
     own_place = pl.ds(y * NZ + HALF, 1)
 
     def load_own(src, dst):
@@ -286,6 +297,8 @@
     rho = rho0 - radius_offset
     scaled = table(types[...], type_scales) * rho
 
+    forward = cells = None
+
     def own_rows(b):
         return [pos[f, b : b + 1, :] for f in range(3)]
 
@@ -294,6 +307,12 @@
         return dx, dy, dz, dx * dx + dy * dy + dz * dz
 
     def own_descreen():
+        nonlocal forward, cells
+        ids = lax.broadcasted_iota(I32, (16, ATOMS), 0) * ATOMS + lax.broadcasted_iota(I32, (16, ATOMS), 1)
+        held = owners[...]
+        base = r * REGION_BLOCKS + d * BLK
+        cells = [jnp.sum(jnp.where(held == base + b, ids, 0).astype(F32)) for b in range(BLK)]
+        forward = listed_codes(r, d, pairs, owners_s)
         for b in range(BLK):
             rho_b = rho[b : b + 1]
             spread(own_rows(b) + [rho_b, 8.0 / rho_b], [home1.at[b, f] for f in range(5)])
@@ -306,7 +325,7 @@
 
     load_own(x1, fields)
     pl.semaphore_wait(barrier, len(everyone))
-    gather_body(peers, fields, *sems[:GATHER_SEMS], own_descreen)
+    gather_body(peers, DIRECT1, fields, *sems[:GATHER_SEMS], own_descreen)
 
     previous = 2 - r % 2
     for half, start in enumerate((0, previous * NDEV)):
@@ -398,7 +417,7 @@
                 for f in range(5):
                     acc2[b, f, g, :] = terms[f]
 
-    gather_body(peers, radii, *sems[GATHER_SEMS:], while_radii_travel)
+    gather_body(peers, DIRECT2, radii, *sems[GATHER_SEMS:], while_radii_travel)
 
     for b in range(BLK):
 
@@ -428,15 +447,21 @@
 
 
 def whole(positions, charges, types, pairs, owner_map):
-    smem = pl.BlockSpec(memory_space=pltpu.SMEM)
     vmem = pl.BlockSpec(memory_space=pltpu.VMEM)
     square = (ATOMS, ATOMS)
     return pl.pallas_call(
         whole_kernel,
         out_shape=jax.ShapeDtypeStruct((24, ATOMS), F32),
-        in_specs=[smem, smem, vmem, vmem, vmem, vmem],
+        in_specs=[pl.BlockSpec(memory_space=pl.ANY)] * 6,
         out_specs=vmem,
         scratch_shapes=[
+            pltpu.SMEM((BLK, SLOTS), I32),
+            pltpu.SMEM((NREG * REGION_BLOCKS,), I32),
+            pltpu.VMEM((16, ATOMS), I32),
+            pltpu.VMEM((3, BLK, ATOMS), F32),
+            pltpu.VMEM((BLK, ATOMS), F32),
+            pltpu.VMEM((BLK, ATOMS), I32),
+            pltpu.SemaphoreType.DMA((6,)),
             pltpu.VMEM((1, ROWS1, 1, ATOMS), F32),
             pltpu.VMEM((1, ROWS2, 1, ATOMS), F32),
             pltpu.VMEM((3 * NDEV, ROWS1, 1, ATOMS), F32),

time: 72.6 us -> 71 us (0.978)
  Pallas kernels: 71.8 us -> 70.2 us
    pallas_call x1, Pallas kernels: 70.5 us -> 68.8 us  [whole(): pl.pallas_call(whole_kernel, out_shape=jax.ShapeDtypeStruct((24, ATOMS),...]
where the time goes in v4:
time: 71 us; the launch traced here: 70.8 us
  Pallas kernels  70.2 us (99%)
    pallas_call x1, Pallas kernels, whole(): pl.pallas_call(whole_kernel, out_shape=jax.ShapeDtypeStruct((24, ATOMS),...  68.8 us

profile of v4, /device:TPU:1, one launch (start us, length us, event | category | flops | bytes accessed | tf_op | source)
XLA Modules:
  0.0 70.8 jit_solution(11208191029956850676)
XLA Ops:
  0.6 68.8 %whole.1.packed = f32[24,128]{1,0:T(8,128)} custom-call(s32[4,13]{1,0:T(4,128)} %pairs_in.1, s32[2048]{0:T(1024)} %owners_s_in.1, s32[16,128]{1,0:T(8,128)} %bitcast.1, f32[3,4,128]{2,1,0:T(4,128)} %pos_in.1, f32[4,128]{1,0:T(4,128)} %charges_in.1, s32[4,128]{1,0:T(4,128)} %types_in.1), custom_call_target="tpu_custom_call" | custom-call | tf_op jit(solution)/shard_map/whole/pallas_call | solution.py:452
  69.5 1.3 %unpack.1 = (f32[4,128]{1,0:T(4,128)}, f32[4,128]{1,0:T(4,128)}, f32[3,4,128]{2,1,0:T(4,128)}, f32[4,128]{1,0:T(4,128)}) custom-call(f32[24,128]{1,0:T(8,128)} %whole.1.packed), custom_call_target="tpu_custom_call" | custom-call | tf_op jit(solution)/shard_map/unpack/pallas_call | solution.py:500

commit v5 on v4

--- a/solution.py
+++ b/solution.py
@@ -149,8 +149,8 @@
     dma = pltpu.SemaphoreType.DMA
     parts = len(PIECES)
     return [
-        dma((NZ,)),
-        dma((NZ,)),
+        dma((2 * REACH + 2,)),
+        dma((HALF + REACH + 2,)),
         dma((NY - 1, parts)),
         dma((NY - 1, parts)),
         dma((2, NY, parts)),
@@ -238,7 +238,10 @@
             total = total + jnp.where(rank[b * BLK + o : b * BLK + o + 1] == wanted, code, 0.0)
         picked.append(total)
     picked = jnp.concatenate(picked, axis=0)
-    found[...] = jnp.broadcast_to((row_sums(picked) + 0.5).astype(I32), found.shape)
+    codes = (row_sums(picked) + 0.5).astype(I32)
+    for b in range(BLK):
+        for n in range(TILES):
+            found[b, n] = codes[0, b * REV + n]
 
 
 GROUP = 64
@@ -259,7 +262,7 @@
 
 def whole_kernel(
     pairs_in, owners_s_in, owners_in, pos_in, charges_in, types_in, out,
-    pairs, owners_s, owners, pos, charges, types, brought, x1, x2, fields, radii, home1, home2, acc1, acc2, geo, listed, found, found_s, local, *sems
+    pairs, owners_s, owners, pos, charges, types, brought, x1, x2, fields, radii, home1, home2, acc1, acc2, geo, listed, found, local, *sems
 ):
     targets = (pairs, owners_s, owners, pos, charges, types)
     sources = (pairs_in, owners_s_in, owners_in, pos_in, charges_in, types_in)
@@ -325,7 +328,9 @@
 
     load_own(x1, fields)
     pl.semaphore_wait(barrier, len(everyone))
-    gather_body(peers, DIRECT1, fields, *sems[:GATHER_SEMS], own_descreen)
+    first = sems[:GATHER_SEMS]
+    again = [sem for pair in zip(first[::2], sems[GATHER_SEMS:]) for sem in pair]
+    gather_body(peers, DIRECT1, fields, *first, own_descreen)
 
     previous = 2 - r % 2
     for half, start in enumerate((0, previous * NDEV)):
@@ -336,12 +341,9 @@
 
         lax.fori_loop(0, NDEV, take, 0, unroll=16)
     merge_partners(r, forward, cells, listed[...], found)
-    copy = pltpu.make_async_copy(found, found_s, local)
-    copy.start()
-    copy.wait()
 
     def partner(b, n):
-        code = found_s[0, b * REV + n]
+        code = found[b, n]
         where = jnp.clip(code, 1, 3 * REGION_BLOCKS) - 1
         return code > 0, where >> 2, where & (BLK - 1)
 
@@ -417,7 +419,7 @@
                 for f in range(5):
                     acc2[b, f, g, :] = terms[f]
 
-    gather_body(peers, DIRECT2, radii, *sems[GATHER_SEMS:], while_radii_travel)
+    gather_body(peers, DIRECT2, radii, *again, while_radii_travel)
 
     for b in range(BLK):
 
@@ -472,12 +474,11 @@
             pltpu.VMEM((BLK, 5) + square, F32),
             pltpu.VMEM((BLK * TILES, 4) + square, F32),
             pltpu.VMEM(square, F32),
-            pltpu.VMEM((8, ATOMS), I32),
-            pltpu.SMEM((8, ATOMS), I32),
+            pltpu.SMEM((BLK, TILES), I32),
             pltpu.SemaphoreType.DMA,
         ]
         + gather_scratch()
-        + gather_scratch(),
+        + gather_scratch()[1::2],
         compiler_params=pltpu.CompilerParams(
             collective_id=0, has_side_effects=True, vmem_limit_bytes=56 * 1024 * 1024
         ),

time: 71 us -> 70.3 us (level)
  no operation moved by 1% of the time
where the time goes in v5:
time: 70.3 us; the launch traced here: 70.1 us
  Pallas kernels  69.5 us (99%)
    pallas_call x1, Pallas kernels, whole(): pl.pallas_call(whole_kernel, out_shape=jax.ShapeDtypeStruct((24, ATOMS),...  68.2 us

profile of v5, /device:TPU:1, one launch (start us, length us, event | category | flops | bytes accessed | tf_op | source)
XLA Modules:
  0.0 70.1 jit_solution(1077334217249564772)
XLA Ops:
  0.6 68.2 %whole.1.packed = f32[24,128]{1,0:T(8,128)} custom-call(s32[4,13]{1,0:T(4,128)} %pairs_in.1, s32[2048]{0:T(1024)} %owners_s_in.1, s32[16,128]{1,0:T(8,128)} %bitcast.1, f32[3,4,128]{2,1,0:T(4,128)} %pos_in.1, f32[4,128]{1,0:T(4,128)} %charges_in.1, s32[4,128]{1,0:T(4,128)} %types_in.1), custom_call_target="tpu_custom_call" | custom-call | tf_op jit(solution)/shard_map/whole/pallas_call | solution.py:454
  68.8 1.3 %unpack.1 = (f32[4,128]{1,0:T(4,128)}, f32[4,128]{1,0:T(4,128)}, f32[3,4,128]{2,1,0:T(4,128)}, f32[4,128]{1,0:T(4,128)}) custom-call(f32[24,128]{1,0:T(8,128)} %whole.1.packed), custom_call_target="tpu_custom_call" | custom-call | tf_op jit(solution)/shard_map/unpack/pallas_call | solution.py:501
